TPU v7x, 32 devices: a whole 2x2x4 slice. The times are simulated.
32 devices in a mesh: groups: 2 (over y), gx: 4 (over z), gy: 4 (over x, core).
Axes of the slice: x: 2, y: 2, z: 4, core: 2. Of those that a mesh axis runs over, the one named last changes fastest.
Arguments:
- children: float32 [4, 4, 4, 512, 512], P('groups', 'gx', 'gy'), parts along dimension 0, as said below
Outputs:
- merged: float32 [4, 4, 4, 256, 1024], P('groups', 'gx', 'gy'), parts along dimension 0
There are 2 independent parts, one for each index of `groups`. A program takes and returns all parts, laid end to end along the dimension named above; each array names one. Nothing has to cross between parts.
Inputs may be any that keep to these rules, and one draw needn't show every extreme that they name: `children`: every child operator is symmetric, and every sum S formed at either level is symmetric positive definite with smallest eigenvalue at least 1.
All inputs are finite; a program needn't handle non-finite values.
Results may differ from a plain program's by a relative error of at most 0.00005.
Values sent between devices are 32-bit elements; how exact they have to be, the bound alone decides.
No kernel may reach another device: no remote copies, remote signals or barrier semaphores. Data moves between devices by JAX's collectives and lax.ppermute only.
A program may use at most 64 MiB of HBM per device.

v0:
```python
import jax
import jax.numpy as jnp
from jax import lax
from jax.sharding import PartitionSpec as P


def swapped(block, axis, bit):
    count = lax.axis_size(axis)
    route = []
    for low in range(count):
        high = low | 1 << bit
        if high != low and high < count:
            route += [(low, high), (high, low)]
    return lax.ppermute(block, axis, route)


def pick_columns(matrix, order, side_count):
    return jnp.concatenate(
        [matrix[..., block * side_count : (block + 1) * side_count] for block in order], -1
    )


def pick_rows(matrix, order, side_count):
    return jnp.concatenate(
        [matrix[..., block * side_count : (block + 1) * side_count, :] for block in order], -2
    )


def definite_solve(matrix, right_sides):

    def single(one_matrix, one_sides):
        factor = jnp.linalg.cholesky(one_matrix)
        return jax.scipy.linalg.cho_solve((factor, True), one_sides)

    return jax.vmap(single)(matrix, right_sides)


def product(left_part, right_part):
    return jnp.einsum("wij,wjk->wik", left_part, right_part, precision=lax.Precision.HIGHEST)


def body(children):
    child_tiles = children[:, 0, 0]
    side_count = child_tiles.shape[-1] // 4
    count_y = lax.axis_size("gy")
    count_x = lax.axis_size("gx")
    bit_y = count_y.bit_length() - 2
    bit_x = count_x.bit_length() - 2
    is_top = lax.axis_index("gy") >= count_y // 2
    is_right = lax.axis_index("gx") >= count_x // 2
    flipped = pick_rows(
        pick_columns(child_tiles, (0, 1, 3, 2), side_count), (0, 1, 3, 2), side_count
    )
    own_tile = jnp.where(is_top, flipped, child_tiles)
    partner = swapped(child_tiles, "gy", bit_y)
    partner_rows = jnp.where(
        is_top,
        partner[:, 3 * side_count :, :],
        pick_columns(partner[:, 2 * side_count : 3 * side_count, :], (0, 1, 3, 2), side_count),
    )
    interface = (
        own_tile[:, 3 * side_count :, 3 * side_count :] + partner_rows[:, :, 3 * side_count :]
    )
    right_sides = jnp.concatenate(
        [own_tile[:, 3 * side_count :, : 3 * side_count], partner_rows[:, :, : 3 * side_count]], -1
    )
    solution_map = definite_solve(interface, right_sides)
    empty_block = jnp.zeros_like(own_tile[:, : 3 * side_count, : 3 * side_count])
    kept_rows = jnp.concatenate([own_tile[:, : 3 * side_count, : 3 * side_count], empty_block], -1)
    kept_rows = kept_rows - product(own_tile[:, : 3 * side_count, 3 * side_count :], solution_map)
    middle = jnp.where(is_top, pick_columns(kept_rows, (3, 4, 5, 0, 1, 2), side_count), kept_rows)
    left_form = pick_rows(
        pick_columns(middle, (0, 2, 3, 5, 1, 4), side_count), (0, 2, 1), side_count
    )
    right_form = pick_rows(
        pick_columns(middle, (1, 2, 4, 5, 0, 3), side_count), (1, 2, 0), side_count
    )
    arranged = jnp.where(is_right, right_form, left_form)
    my_rows = arranged[:, 2 * side_count :, :]
    other_rows = swapped(my_rows, "gy", bit_y)
    own_box = jnp.where(
        is_top, jnp.concatenate([other_rows, my_rows], 1), jnp.concatenate([my_rows, other_rows], 1)
    )
    sibling = swapped(own_box, "gx", bit_x)
    outer = 4 * side_count
    interface_two = own_box[:, :, outer:] + sibling[:, :, outer:]
    sides_two = jnp.where(
        is_right,
        jnp.concatenate([sibling[:, :, :outer], own_box[:, :, :outer]], -1),
        jnp.concatenate([own_box[:, :, :outer], sibling[:, :, :outer]], -1),
    )
    solution_two = definite_solve(interface_two, sides_two)
    local_block = arranged[:, : 2 * side_count, :outer]
    empty_two = jnp.zeros_like(local_block)
    diagonal_part = jnp.where(
        is_right,
        jnp.concatenate([empty_two, local_block], -1),
        jnp.concatenate([local_block, empty_two], -1),
    )
    result = diagonal_part - product(arranged[:, : 2 * side_count, outer:], solution_two)
    return result[:, None, None]


def solution(mesh):
    placed = (P("groups", "gx", "gy", None, None),)
    return jax.shard_map(
        body,
        mesh=mesh,
        in_specs=placed,
        out_specs=P("groups", "gx", "gy", None, None),
        check_vma=False,
    )
```

profile of v0, /device:TPU:0, one launch (start us, length us, event | category | flops | bytes accessed | tf_op | source)
XLA Modules:
  0.0 335.1 jit_solution(2703248917000696313)
XLA Ops:
  0.0 1.9 copy.17
  1.9 3.0 collective-permute-start
  6.1 1.1 slice.276
  7.2 2.0 fusion.3
  9.2 0.9 slice.285
  10.1 0.6 copy-done
  10.8 39.9 %collective-permute-done = f32[2,512,512]{1,2,0:T(8,128)} collective-permute-done((f32[2,512,512]{1,2,0:T(8,128)S(1)}, f32[2,512,512]{1,2,0:T(8,128)}, u32[]{:S(2)}, u32[]{:S(2)}) %collective-permute-start) | collective-permute-done | bytes 2097184 | tf_op jit(solution)/shard_map/ppermute | solution.py:14
  50.7 1.0 fusion.39
  51.7 1.0 slice.281
  52.7 1.1 slice_select_fusion
  53.8 0.9 slice_add_fusion.1
  55.0 23.5 %custom-call.31 = f32[2,128,128]{2,1,0:T(8,128)S(1)} custom-call(f32[2,128,128]{2,1,0:T(8,128)S(1)} %copy.19), custom_call_target="Cholesky" | custom-call | tf_op jit(solution)/shard_map/vmap(jit(cholesky))/cholesky | solution.py:32
  78.7 19.8 %custom-call.32 = f32[2,1,128,128]{2,3,1,0:T(8,128)S(1)} custom-call(f32[2,1,128,128]{3,2,1,0:T(8,128)S(1)} %select_bitcast_fusion.1), custom_call_target="InvertDiagBlocksLowerTriangular" | custom-call | tf_op jit(solution)/shard_map/vmap(jit(_cho_solve))/triangular_solve | solution.py:33
  98.6 0.9 fusion.15
  99.5 0.8 fusion.25
  100.3 3.1 pad_subtract_fusion
  104.9 1.8 collective-permute-start.1
  106.7 17.0 %collective-permute-done.1 = f32[2,128,768]{1,2,0:T(8,128)S(1)} collective-permute-done((f32[2,128,768]{1,2,0:T(8,128)S(1)}, f32[2,128,768]{1,2,0:T(8,128)S(1)}, u32[]{:S(2)}, u32[]{:S(2)}) %collective-permute-start.1) | collective-permute-done | bytes 786464 | tf_op jit(solution)/shard_map/ppermute | solution.py:14
  123.6 1.2 maximum_select_fusion.2
  124.9 2.5 collective-permute-start.2
  127.4 1.1 slice.301
  128.5 2.3 slice.307
  130.8 63.7 %collective-permute-done.2 = f32[2,256,768]{1,2,0:T(8,128)} collective-permute-done((f32[2,256,768]{1,2,0:T(8,128)}, f32[2,256,768]{1,2,0:T(8,128)}, u32[]{:S(2)}, u32[]{:S(2)}) %collective-permute-start.2) | collective-permute-done | bytes 1572896 | tf_op jit(solution)/shard_map/ppermute | solution.py:14
  194.5 1.3 slice_add_fusion
  196.0 0.8 copy-done.7
  196.8 23.5 %custom-call.33 = f32[2,128,128]{2,1,0:T(8,128)S(1)} custom-call(f32[2,128,128]{2,1,0:T(8,128)S(1)} %cholesky.131), custom_call_target="Cholesky" | custom-call | tf_op jit(solution)/shard_map/vmap(jit(cholesky))/cholesky | solution.py:32
  220.4 19.9 %custom-call.34 = f32[2,1,128,128]{2,3,1,0:T(8,128)S(1)} custom-call(f32[2,1,128,128]{3,2,1,0:T(8,128)S(1)} %select_bitcast_fusion), custom_call_target="InvertDiagBlocksLowerTriangular" | custom-call | tf_op jit(solution)/shard_map/vmap(jit(cholesky))/cholesky | solution.py:32
  240.3 1.2 constant_dynamic-update-slice_fusion.2
  241.4 1.3 convolution_subtract_fusion.1
  242.8 23.5 %custom-call.35 = f32[2,128,128]{2,1,0:T(8,128)S(1)} custom-call(f32[2,128,128]{2,1,0:T(8,128)S(1)} %convolution_subtract_fusion.1), custom_call_target="Cholesky" | custom-call | tf_op jit(solution)/shard_map/vmap(jit(cholesky))/cholesky | solution.py:32
  266.4 0.6 copy-done.6
  267.1 2.1 select_select_fusion
  269.2 7.2 %while.1 = (s32[]{:T(128)}, f32[2,256,256]{2,1,0:T(8,128)}, s32[2,2]{1,0:T(2,128)S(1)}, f32[2,2,128,128]{3,2,0,1:T(8,128)}, s32[]{:T(128)}) while((s32[]{:T(128)}, f32[2,256,256]{2,1,0:T(8,128)}, s32[2,2]{1,0:T(2,128)S(1)}, f32[2,2,128,128]{3,2,0,1:T(8,128)}, s32[]{:T(128)}) %tuple.32), condition=%wide.while_cond, body=%wide.while_body.sunk | while | flops 2 | bytes 263777 | solution.py:33
  269.2 0.6 fusion.50
  269.8 3.0 bitcast_dynamic-update-slice_fusion.2
  272.8 0.6 fusion.50
  273.5 2.9 bitcast_dynamic-update-slice_fusion.2
  276.4 41.0 %custom-call.36 = f32[2,2,128,128]{2,3,1,0:T(8,128)} custom-call(f32[2,2,128,128]{3,2,1,0:T(8,128)} %bitcast.62), custom_call_target="InvertDiagBlocksLowerTriangular" | custom-call | tf_op jit(solution)/shard_map/vmap(jit(_cho_solve))/triangular_solve | solution.py:33
  317.4 1.3 slice.306
  319.0 0.7 copy-done.9
  319.7 1.1 fusion.13
  320.7 1.8 fusion.32
  322.6 1.1 fusion.12
  323.7 1.0 fusion.30
  324.7 1.1 convolution_subtract_fusion
  325.8 1.0 fusion.29
  326.8 5.0 %subtract_bitcast_fusion = f32[2,1,1,256,1024]{3,4,0,2,1:T(8,128)} fusion(f32[2,256,512]{1,2,0:T(8,128)S(1)} %copy-done.4, f32[2,128,1024]{2,1,0:T(8,128)S(1)} %fusion.30, f32[2,128,1024]{2,1,0:T(8,128)S(1)} %fusion.29, pred[]{:T(512)S(6)} %ge.10, f32[2,384,768]{1,2,0:T(8,128)S(1)} %fusion.1), kind=kOutput, calls=%fused_computation.26 | convolution fusion | flops 1612185600 | bytes 5767169 | tf_op jit(solution)/shard_map/wij,wjk->wik/dot_general | solution.py:39
  331.8 2.9 copy.31
  (56 shorter events, 4.1 us)
Async XLA Ops:
  1.9 48.7 %collective-permute-start = (f32[2,512,512]{1,2,0:T(8,128)S(1)}, f32[2,512,512]{1,2,0:T(8,128)}, u32[]{:S(2)}, u32[]{:S(2)}) collective-permute-start(f32[2,512,512]{1,2,0:T(8,128)S(1)} %bitcast.59), channel_id=1, source_target_pairs={{0,2},{2,0},{1,3},{3,1},{4,6},{6,4},{5,7},{7,5},{8,10},{10,8},{9,1... | collective-permute-start | bytes 6291464 | tf_op jit(solution)/shard_map/ppermute | solution.py:14
  5.1 0.8 copy-start.1
  5.1 1.0 copy-start.2
  9.2 1.5 copy-start
  52.6 45.9 %copy-start.8 = (f32[2,128,384]{1,2,0:T(8,128)S(1)}, f32[2,128,384]{1,2,0:T(8,128)}, u32[]{:S(2)}) copy-start(f32[2,128,384]{1,2,0:T(8,128)} %slice.285) | copy-start | bytes 1179652
  104.9 18.8 %collective-permute-start.1 = (f32[2,128,768]{1,2,0:T(8,128)S(1)}, f32[2,128,768]{1,2,0:T(8,128)S(1)}, u32[]{:S(2)}, u32[]{:S(2)}) collective-permute-start(f32[2,128,768]{1,2,0:T(8,128)S(1)} %slice.303), channel_id=1, source_target_pairs={{0,2},{2,0},{1,3},{3,1},{4,6},{6,4},{5,7},{7,5},{8,10},{10,8},{9,1... | collective-permute-start | bytes 2359304 | tf_op jit(solution)/shard_map/ppermute | solution.py:14
  124.9 69.6 %collective-permute-start.2 = (f32[2,256,768]{1,2,0:T(8,128)}, f32[2,256,768]{1,2,0:T(8,128)}, u32[]{:S(2)}, u32[]{:S(2)}) collective-permute-start(f32[2,256,768]{1,2,0:T(8,128)} %maximum_select_fusion.2), channel_id=1, source_target_pairs={{0,8},{8,0},{4,12},{12,4},{1,9},{9,1},{5,13},{13,5},{2,10},{10,2},... | collective-permute-start | bytes 4718600 | tf_op jit(solution)/shard_map/ppermute | solution.py:14
  196.0 0.8 copy-start.7
  266.3 0.8 copy-start.6
  267.0 51.6 %copy-start.3 = (f32[2,256,512]{1,2,0:T(8,128)S(1)}, f32[2,256,512]{1,2,0:T(8,128)}, u32[]{:S(2)}) copy-start(f32[2,256,512]{1,2,0:T(8,128)} %slice.307) | copy-start | bytes 3145732
  318.7 1.0 copy-start.9
  319.7 1.1 copy-start.5
  324.7 2.1 copy-start.4
where the time goes:
time: 342 us; the launch traced here: 335 us
  other arithmetic  161 us (47%)
  waiting for transfers between devices  121 us (35%)
  local copies, waits for them, and re-layouts  25.6 us (7%)
  matrix products  19.2 us (6%)
  starting transfers between devices  7.33 us (2%)
    ppermute x3, waiting for transfers between devices, swapped(): return lax.ppermute(block, axis, route)  121 us
    another operation x11, other arithmetic, single(): factor = jnp.linalg.cholesky(one_matrix)  90.6 us
    another operation x7, other arithmetic, single(): return jax.scipy.linalg.cho_solve((factor, True), one_sides)  63 us
    another operation x8, matrix products, single(): return jax.scipy.linalg.cho_solve((factor, True), one_sides)  8.7 us
    dot_general x2, matrix products, product(): jnp.einsum('wij,wjk->wik', left_part, right_part, precision=lax.Precision...  8.06 us
    ppermute x3, starting transfers between devices, swapped(): return lax.ppermute(block, axis, route)  7.33 us
    another operation x6, local copies, waits for them, and re-layouts  7.24 us
  transfers between devices with their start and end apart: 3, of which 3 were waited for; matrix products, arithmetic and copies ran while one was open for 2% of the time, Pallas kernels for 0%

commit v1 on v0

v1 whole, which is shorter than its diff:
```python
import functools

import jax
import jax.numpy as jnp
from jax import lax
from jax.experimental import pallas as pl
from jax.experimental.pallas import tpu as pltpu
from jax.sharding import PartitionSpec as P

SUB = 8


def swapped(block, axis):
    count = lax.axis_size(axis)
    bit = count.bit_length() - 2
    route = []
    for low in range(count):
        high = low | 1 << bit
        if high != low and high < count:
            route += [(low, high), (high, low)]
    return lax.ppermute(block, axis, route)


def after(block, other):
    return lax.optimization_barrier((block, other))[0]


def role():
    right = (lax.axis_index("gx") >= lax.axis_size("gx") // 2).astype(jnp.int32)
    top = (lax.axis_index("gy") >= lax.axis_size("gy") // 2).astype(jnp.int32)
    return right, top


def mul(a, b):
    return lax.dot_general(
        a, b, (((1,), (0,)), ((), ())), precision=lax.Precision.HIGHEST, preferred_element_type=jnp.float32
    )


def mul_t(a, b):
    return lax.dot_general(
        a, b, (((0,), (0,)), ((), ())), precision=lax.Precision.HIGHEST, preferred_element_type=jnp.float32
    )


def tree(terms):
    while len(terms) > 1:
        terms = [terms[i] + terms[i + 1] for i in range(0, len(terms) - 1, 2)] + terms[len(terms) & ~1 :]
    return terms[0]


def inverses(matrices):
    size = matrices[0].shape[0]
    panels = size // SUB
    many = len(matrices)
    lane = lax.broadcasted_iota(jnp.int32, (SUB, size), 1)
    sub = lax.broadcasted_iota(jnp.int32, (SUB, size), 0)
    full = lambda v: jnp.broadcast_to(v, (SUB, size))
    state = [[m[SUB * i : SUB * i + SUB, :] for i in range(panels)] for m in matrices]
    lower = [[] for _ in matrices]
    scaled = [[] for _ in matrices]
    for p in range(panels):
        first = SUB * p
        inside = (lane >= first) & (lane < first + SUB)
        unit = lane - first == sub
        done = lane < first + SUB
        blocks = [[full(state[w][p][:, first + j : first + j + 1]) for j in range(SUB)] for w in range(many)]
        for k in range(SUB):
            at_row = sub == k
            for w in range(many):
                old = blocks[w]
                pivot = old[k]
                inverse = 1.0 / full(pivot[k : k + 1, :])
                new = []
                for j in range(SUB):
                    if j == k:
                        new.append(jnp.where(at_row, inverse, -pivot * inverse))
                    else:
                        scaled_row = full(old[j][k : k + 1, :]) * inverse
                        new.append(jnp.where(at_row, scaled_row, old[j] - pivot * scaled_row))
                blocks[w] = new
        for w in range(many):
            rows = state[w]
            panel = jnp.where(inside, jnp.where(unit, 1.0, 0.0), rows[p])
            gained = tree([blocks[w][l] * full(panel[l : l + 1, :]) for l in range(SUB)])
            lower[w].append(jnp.where(done, panel, 0.0))
            scaled[w].append(jnp.where(done, gained, 0.0))
            spread = [full(gained[l : l + 1, :]) for l in range(SUB)]
            for i in range(p + 1, panels):
                row = rows[i]
                change = tree([full(row[:, first + l : first + l + 1]) * spread[l] for l in range(SUB)])
                rows[i] = jnp.where(inside, 0.0, row) - change
    return [mul_t(jnp.concatenate(lower[w], 0), jnp.concatenate(scaled[w], 0)) for w in range(many)]


def square_masks(side):
    row = lax.broadcasted_iota(jnp.int32, (side, side), 0)
    col = lax.broadcasted_iota(jnp.int32, (side, side), 1)
    return row > col, row == col


def pack_yy(square):
    below, diag = square_masks(square.shape[0])
    return jnp.where(below | diag, square, square.T)


def pack_xx(square, line):
    below, diag = square_masks(square.shape[0])
    return jnp.where(diag, jnp.broadcast_to(line, square.shape), jnp.where(below, square.T, square))


def interface_kernel(side, tiles, pack, own_yy, own_xx, sems):
    right, top = role()
    side_y = 3 - top
    side_x = 1 - right
    waves = pack.shape[0]

    def piece(w, row_side, col_side):
        rows = pl.ds(pl.multiple_of(row_side * side, side), side)
        cols = pl.ds(pl.multiple_of(col_side * side, side), side)
        return tiles.at[w, rows, cols]

    copies = []
    for w in range(waves):
        copies += [
            pltpu.make_async_copy(piece(w, side_y, side_y), own_yy.at[w], sems.at[3 * w]),
            pltpu.make_async_copy(piece(w, side_x, side_x), own_xx.at[w], sems.at[3 * w + 1]),
            pltpu.make_async_copy(piece(w, side_y, side_x), pack.at[w, pl.ds(side, side), :], sems.at[3 * w + 2]),
        ]
    for copy in copies:
        copy.start()
    below, diag = square_masks(side)
    for w in range(waves):
        copies[3 * w].wait()
        copies[3 * w + 1].wait()
        xx = own_xx[w]
        pack[w, 0:side, :] = jnp.where(below | diag, own_yy[w], xx)
        line = jnp.sum(jnp.where(diag, xx, 0.0), 0, keepdims=True)
        pack[w, 2 * side :, :] = jnp.broadcast_to(line, (SUB, side))
    for w in range(waves):
        copies[3 * w + 2].wait()


def interfaces(tiles):
    waves, side = tiles.shape[0], tiles.shape[1] // 4
    return pl.pallas_call(
        functools.partial(interface_kernel, side),
        name="interfaces",
        out_shape=jax.ShapeDtypeStruct((waves, 2 * side + SUB, side), jnp.float32),
        in_specs=[pl.BlockSpec(memory_space=pl.ANY)],
        out_specs=pl.BlockSpec(memory_space=pltpu.VMEM),
        scratch_shapes=[
            pltpu.VMEM((waves, side, side), jnp.float32),
            pltpu.VMEM((waves, side, side), jnp.float32),
            pltpu.SemaphoreType.DMA((3 * waves,)),
        ],
        cost_estimate=pl.CostEstimate(flops=0, bytes_accessed=5 * waves * side * side * 4, transcendentals=0),
    )(tiles)


def coupling_kernel(side, tiles, whole, first, second, third, sems):
    right, top = role()
    rows_of = (3 - top, 1 - right)
    cols_of = (right, 2 + top)
    copies = []
    for w in range(2):
        for i in range(2):
            rows = pl.ds(pl.multiple_of(rows_of[i] * side, side), side)
            here = pl.ds(i * side, side)
            for j in range(2):
                cols = pl.ds(pl.multiple_of(cols_of[j] * side, side), side)
                source = tiles.at[w, rows, cols]
                there = pl.ds(j * side, side)
                n = len(copies)
                copies.append(pltpu.make_async_copy(source, whole.at[w, here, there], sems.at[n]))
                if w == 0:
                    target = first.at[here, there]
                else:
                    target = (second, third)[j].at[here, :]
                copies.append(pltpu.make_async_copy(source, target, sems.at[n + 1]))
    for copy in copies:
        copy.start()
    for copy in copies:
        copy.wait()


def couplings(tiles):
    waves, side = tiles.shape[0], tiles.shape[1] // 4
    shapes = [(waves, 2 * side, 2 * side), (2 * side, 2 * side), (2 * side, side), (2 * side, side)]
    return pl.pallas_call(
        functools.partial(coupling_kernel, side),
        name="couplings",
        out_shape=[jax.ShapeDtypeStruct(s, jnp.float32) for s in shapes],
        in_specs=[pl.BlockSpec(memory_space=pl.ANY)],
        out_specs=[pl.BlockSpec(memory_space=pltpu.VMEM)] * 4,
        scratch_shapes=[pltpu.SemaphoreType.DMA((8 * waves,))],
        cost_estimate=pl.CostEstimate(flops=0, bytes_accessed=16 * waves * side * side * 4, transcendentals=0),
    )(tiles)


def first_kernel(side, own, mate, coupling, blocks, sides):
    waves = own.shape[0]
    sums = [pack_yy(own[w, 0:side, :] + mate[w, 0:side, :]) for w in range(waves)]
    inverse = inverses(sums)
    for w in range(waves):
        own_yx = own[w, side : 2 * side, :]
        mate_yu = mate[w, side : 2 * side, :]
        gain_x = mul(inverse[w], own_yx)
        gain_u = mul(inverse[w], mate_yu)
        blocks[w, 0] = gain_x
        blocks[w, 1] = gain_u
        blocks[w, 2] = pack_xx(own[w, 0:side, :], own[w, 2 * side : 2 * side + 1, :]) - mul_t(own_yx, gain_x)
        blocks[w, 3] = -mul_t(own_yx, gain_u)
        blocks[w, 4] = pack_xx(mate[w, 0:side, :], mate[w, 2 * side : 2 * side + 1, :]) - mul_t(mate_yu, gain_u)
        side_y = coupling[w, 0:side, :]
        sides[w, 0] = mul(inverse[w], side_y)
        sides[w, 1] = coupling[w, side:, :] - mul_t(gain_x, side_y)
        sides[w, 2] = -mul_t(gain_u, side_y)


def second_kernel(side, pack, one, sides_one, blocks, sides):
    waves = pack.shape[0]
    sums = [
        one[w, 2] + pack_xx(pack[w, 0:side, :], pack[w, 2 * side : 2 * side + 1, :]) for w in range(waves)
    ]
    inverse = inverses(sums)
    for w in range(waves):
        vx = pack[w, side : 2 * side, :]
        xu = one[w, 3]
        gain_v = mul(inverse[w], vx.T)
        gain_u = mul(inverse[w], xu)
        blocks[w, 0] = gain_v
        blocks[w, 1] = gain_u
        blocks[w, 2] = pack_yy(pack[w, 0:side, :]) - mul(vx, gain_v)
        blocks[w, 3] = -mul(vx, gain_u)
        blocks[w, 4] = one[w, 4] - mul_t(xu, gain_u)
        side_x = sides_one[w, 1]
        sides[w, 0] = mul(inverse[w], side_x)
        sides[w, 1] = -mul_t(gain_v, side_x)
        sides[w, 2] = sides_one[w, 2] - mul_t(gain_u, side_x)


def third_kernel(side, pack, one, sides_one, two, sides_two, held):
    waves = pack.shape[0]
    inverse_v = inverses([two[w, 2] + pack_yy(pack[w, 0:side, :]) for w in range(waves)])
    vu = [two[w, 3] + pack[w, side : 2 * side, :] for w in range(waves)]
    gain = [mul(inverse_v[w], vu[w]) for w in range(waves)]
    inverse_u = inverses(
        [
            two[w, 4]
            + pack_xx(pack[w, 0:side, :], pack[w, 2 * side : 2 * side + 1, :])
            - mul_t(vu[w], gain[w])
            for w in range(waves)
        ]
    )
    for w in range(waves):
        side_v = sides_two[w, 1]
        side_u = sides_two[w, 2] - mul_t(gain[w], side_v)
        held_u = mul(inverse_u[w], side_u)
        held_v = mul(inverse_v[w], side_v) - mul(gain[w], held_u)
        held_x = sides_two[w, 0] - mul(two[w, 0], held_v) - mul(two[w, 1], held_u)
        held_y = sides_one[w, 0] - mul(one[w, 0], held_x) - mul(one[w, 1], held_u)
        held[w, 0] = held_y
        held[w, 1] = held_x
        held[w, 2] = held_v
        held[w, 3] = held_u


def whole_call(kernel, name, shapes, flops):
    return lambda *args: pl.pallas_call(
        kernel,
        name=name,
        out_shape=[jax.ShapeDtypeStruct(s, jnp.float32) for s in shapes],
        in_specs=[pl.BlockSpec(memory_space=pltpu.VMEM)] * len(args),
        out_specs=[pl.BlockSpec(memory_space=pltpu.VMEM)] * len(shapes),
        compiler_params=pltpu.CompilerParams(vmem_limit_bytes=32 << 20),
        cost_estimate=pl.CostEstimate(flops=flops, bytes_accessed=1 << 20, transcendentals=0),
    )(*args)


def near_kernel(side, tiles, held, own, mate, cross, far, out, diagonal, buffer, load_sems, sems):
    right, top = role()
    sides = (right, 2 + top)
    loads = []
    for w in range(2):
        for i in range(2):
            rows = pl.ds(pl.multiple_of(sides[i] * side, side), side)
            for j in range(2):
                cols = pl.ds(pl.multiple_of(sides[j] * side, side), side)
                loads.append(
                    pltpu.make_async_copy(
                        tiles.at[w, rows, cols],
                        diagonal.at[w, pl.ds(i * side, side), pl.ds(j * side, side)],
                        load_sems.at[len(loads)],
                    )
                )
                loads[-1].start()
    stores = []

    def put(n, w, slot, value):
        buffer[n] = value
        column = pl.multiple_of(slot * 2 * side, 2 * side)
        stores.append(pltpu.make_async_copy(buffer.at[n], out.at[w, :, pl.ds(column, 2 * side)], sems.at[n]))
        stores[-1].start()

    mate_slot = 2 * right + 1 - top
    cross_slot = 2 * (1 - right) + top
    far_slot = 2 * (1 - right) + 1 - top
    for w in range(2):
        value = -mul_t(held[w, 0], mate[w, 0:side, :]) - mul_t(held[w, 3], mate[w, side:, :])
        put(2 * w, w, mate_slot, value)
    put(4, 0, cross_slot, -mul_t(held[0, 2], cross[0:side, :]) - mul_t(held[0, 1], cross[side:, :]))
    put(5, 0, far_slot, -mul_t(held[0, 2], far[0:side, :]) - mul_t(held[0, 3], far[side:, :]))
    for load in loads:
        load.wait()
    for w in range(2):
        value = diagonal[w] - mul_t(held[w, 0], own[w, 0:side, :]) - mul_t(held[w, 1], own[w, side:, :])
        put(2 * w + 1, w, 2 * right + top, value)
    for store in stores:
        store.wait()


def near_call(tiles, held, own, mate, cross, far):
    waves, side = tiles.shape[0], tiles.shape[1] // 4
    vmem = pl.BlockSpec(memory_space=pltpu.VMEM)
    return pl.pallas_call(
        functools.partial(near_kernel, side),
        name="near_columns",
        out_shape=jax.ShapeDtypeStruct((waves, 2 * side, 8 * side), jnp.float32),
        in_specs=[pl.BlockSpec(memory_space=pl.ANY)] + [vmem] * 5,
        out_specs=pl.BlockSpec(memory_space=pl.ANY),
        scratch_shapes=[
            pltpu.VMEM((waves, 2 * side, 2 * side), jnp.float32),
            pltpu.VMEM((3 * waves, 2 * side, 2 * side), jnp.float32),
            pltpu.SemaphoreType.DMA((4 * waves,)),
            pltpu.SemaphoreType.DMA((3 * waves,)),
        ],
        compiler_params=pltpu.CompilerParams(vmem_limit_bytes=32 << 20),
        cost_estimate=pl.CostEstimate(flops=12 * (2 * side) ** 3, bytes_accessed=1 << 20, transcendentals=0),
    )(tiles, held, own, mate, cross, far)


def last_kernel(side, before, held, cross_a, cross_b, far_a, far_b, out, buffer, sems):
    del before
    right, top = role()
    cross_slot = 2 * (1 - right) + top
    far_slot = 2 * (1 - right) + 1 - top
    stores = []
    for n, (slot, near, start, block) in enumerate(
        (
            (cross_slot, 1, 0, cross_a),
            (far_slot, 3, 0, far_a),
            (cross_slot, 1, side, cross_b),
            (far_slot, 3, side, far_b),
        )
    ):
        buffer[n] = -mul_t(held[1, 2], block[0:side, :]) - mul_t(held[1, near], block[side:, :])
        column = pl.multiple_of(slot * 2 * side + start, side)
        stores.append(pltpu.make_async_copy(buffer.at[n], out.at[1, :, pl.ds(column, side)], sems.at[n]))
        stores[-1].start()
    for store in stores:
        store.wait()


def last_call(before, held, *pieces):
    side = held.shape[2]
    vmem = pl.BlockSpec(memory_space=pltpu.VMEM)
    return pl.pallas_call(
        functools.partial(last_kernel, side),
        name="last_columns",
        out_shape=jax.ShapeDtypeStruct(before.shape, jnp.float32),
        in_specs=[pl.BlockSpec(memory_space=pl.ANY)] + [vmem] * 5,
        out_specs=pl.BlockSpec(memory_space=pl.ANY),
        scratch_shapes=[
            pltpu.VMEM((4, 2 * side, side), jnp.float32),
            pltpu.SemaphoreType.DMA((4,)),
        ],
        input_output_aliases={0: 0},
        compiler_params=pltpu.CompilerParams(vmem_limit_bytes=32 << 20),
        cost_estimate=pl.CostEstimate(flops=4 * (2 * side) ** 3, bytes_accessed=1 << 20, transcendentals=0),
    )(before, held, *pieces)


def body(children):
    tiles = children[:, 0, 0]
    waves, side = tiles.shape[0], tiles.shape[1] // 4
    pack = interfaces(tiles)
    whole, *parts = couplings(tiles)
    mate_pack = swapped(pack, "gy")
    cross_pack = swapped(pack, "gx")
    far_pack = swapped(cross_pack, "gy")
    mate = swapped(whole, "gy")
    previous = cross_pack
    cross = []
    far = []
    for part in parts:
        previous = swapped(after(part, previous), "gx")
        cross.append(previous)
        far.append(swapped(previous, "gy"))
    square = side * side
    matrix, sides = (waves, 5, side, side), (waves, 3, side, 2 * side)
    one, sides_one = whole_call(
        functools.partial(first_kernel, side), "eliminate_y", [matrix, sides], 20 * waves * square * side
    )(pack, mate_pack, whole)
    two, sides_two = whole_call(
        functools.partial(second_kernel, side), "eliminate_x", [matrix, sides], 20 * waves * square * side
    )(cross_pack, one, sides_one)
    (held,) = whole_call(
        functools.partial(third_kernel, side),
        "eliminate_far",
        [(waves, 4, side, 2 * side)],
        40 * waves * square * side,
    )(far_pack, one, sides_one, two, sides_two)
    near = near_call(tiles, held, whole, mate, cross[0], far[0])
    merged = last_call(near, held, cross[1], cross[2], far[1], far[2])
    return merged[:, None, None]


def solution(mesh):
    placed = (P("groups", "gx", "gy", None, None),)
    return jax.shard_map(
        body,
        mesh=mesh,
        in_specs=placed,
        out_specs=P("groups", "gx", "gy", None, None),
        check_vma=False,
    )
```

time: 342 us -> 90.3 us (0.26); the launches traced: 335 us -> 90 us
  other arithmetic: 161 us -> 0 us
  waiting for transfers between devices: 121 us -> 34.5 us
  Pallas kernels: 0 us -> 43.8 us
  local copies, waits for them, and re-layouts: 25.6 us -> 1.05 us
  matrix products: 19.2 us -> 0 us
    another operation x18 -> x0, other arithmetic: 154 us -> none  [the longest x11 90.6 us: single(): factor = jnp.linalg.cholesky(one_matrix)]
    ppermute x3 -> x10, waiting for transfers between devices: 121 us -> 34.5 us  [swapped(): return lax.ppermute(block, axis, route)]
    pallas_call x0 -> x7, Pallas kernels: none -> 43.8 us  [the longest x3 34.1 us: whole_call(): pl.pallas_call(kernel, name=name, out_shape=[jax.ShapeDtypeStruct(s, jnp....]
    another operation x10 -> x0, matrix products: 11.2 us -> none  [the longest x8 8.7 us: single(): return jax.scipy.linalg.cho_solve((factor, True), one_sides)]
    slice x15 -> x0, local copies, waits for them, and re-layouts: 9.32 us -> none  [the longest x1 2.28 us: body(): own_box[:, :, :outer]]
    dot_general x2 -> x0, matrix products: 8.06 us -> none  [product(): jnp.einsum('wij,wjk->wik', left_part, right_part, precision=lax.Precision...]
    another operation x9 -> x0, local copies, waits for them, and re-layouts: 7.35 us -> none
    select_n x6 -> x0, other arithmetic: 5.1 us -> none  [the longest x1 1.99 us: body(): own_tile = jnp.where(is_top, flipped, child_tiles)]
  transfers between devices with their start and end apart: 3 -> 10, of which waited for: 3 -> 4; matrix products, arithmetic and copies ran while one was open for 2% -> 0% of each run, Pallas kernels for 0% -> 45%
where the time goes in v1:
time: 90.3 us; the launch traced here: 90 us
  Pallas kernels  43.8 us (49%)
  waiting for transfers between devices  34.5 us (38%)
  starting transfers between devices  10.4 us (12%)
  local copies, waits for them, and re-layouts  1.05 us (1%)
    ppermute x10, waiting for transfers between devices, swapped(): return lax.ppermute(block, axis, route)  34.5 us
    pallas_call x3, Pallas kernels, whole_call(): pl.pallas_call(kernel, name=name, out_shape=[jax.ShapeDtypeStruct(s, jnp....  34.1 us
    ppermute x10, starting transfers between devices, swapped(): return lax.ppermute(block, axis, route)  10.4 us
    pallas_call x1, Pallas kernels, near_call(): pl.pallas_call(functools.partial(near_kernel, side), name='near_columns',...  3.82 us
    pallas_call x1, Pallas kernels, couplings(): pl.pallas_call(functools.partial(coupling_kernel, side), name='couplings'...  2.36 us
  transfers between devices with their start and end apart: 10, of which 4 were waited for; matrix products, arithmetic and copies ran while one was open for 0% of the time, Pallas kernels for 45%

profile of v1, /device:TPU:0, one launch (start us, length us, event | category | flops | bytes accessed | tf_op | source)
XLA Modules:
  0.0 90.0 jit_solution(9725603023472857980)
XLA Ops:
  0.0 1.8 %interfaces.1.own = f32[2,264,128]{2,1,0:T(8,128)} custom-call(f32[2,512,512]{2,1,0:T(8,128)} %bitcast.4), custom_call_target="tpu_custom_call" | custom-call | bytes 655360 | tf_op jit(solution)/shard_map/interfaces/pallas_call | solution.py:146
  1.8 0.0 copy-start.2
  1.8 4.1 %collective-permute-start = (f32[2,264,128]{2,1,0:T(8,128)}, f32[2,264,128]{2,1,0:T(8,128)S(1)}, u32[]{:S(2)}, u32[]{:S(2)}) collective-permute-start(f32[2,264,128]{2,1,0:T(8,128)} %interfaces.1.own), channel_id=1, source_target_pairs={{0,8},{8,0},{4,12},{12,4},{1,9},{9,1},{5,13},{13,5},{2,10},{10,2},... | collective-permute-start | bytes 811016 | tf_op jit(solution)/shard_map/ppermute | solution.py:21
  5.9 2.4 %couplings.1 = (f32[2,256,256]{2,1,0:T(8,128)}, f32[256,256]{1,0:T(8,128)}, f32[256,128]{1,0:T(8,128)}, f32[256,128]{1,0:T(8,128)}) custom-call(f32[2,512,512]{2,1,0:T(8,128)} %bitcast.5), custom_call_target="tpu_custom_call" | custom-call | bytes 2097152 | tf_op jit(solution)/shard_map/couplings/pallas_call | solution.py:190
  8.3 10.1 %collective-permute-done.pack = f32[2,264,128]{2,1,0:T(8,128)S(1)} collective-permute-done((f32[2,264,128]{2,1,0:T(8,128)}, f32[2,264,128]{2,1,0:T(8,128)S(1)}, u32[]{:S(2)}, u32[]{:S(2)}) %collective-permute-start) | collective-permute-done | bytes 270368 | tf_op jit(solution)/shard_map/ppermute | solution.py:21
  18.4 0.0 collective-permute-start.4
  18.4 1.5 %collective-permute-start.3 = (f32[2,256,256]{2,1,0:T(8,128)}, f32[2,256,256]{2,1,0:T(8,128)S(1)}, u32[]{:S(2)}, u32[]{:S(2)}) collective-permute-start(f32[2,256,256]{2,1,0:T(8,128)} %get-tuple-element.16.coupling.own), channel_id=1, source_target_pairs={{0,2},{2,0},{1,3},{3,1},{4,6},{6,4},{5,7},{7,5},{8,10},{10,8},{9,1... | collective-permute-start | bytes 1572872 | tf_op jit(solution)/shard_map/ppermute | solution.py:21
  19.9 0.0 copy-done.2
  19.9 0.5 collective-permute-start.2
  20.4 12.2 %collective-permute-done.4.cross = f32[256,256]{1,0:T(8,128)S(1)} collective-permute-done((f32[256,256]{1,0:T(8,128)}, f32[256,256]{1,0:T(8,128)S(1)}, u32[]{:S(2)}, u32[]{:S(2)}) %collective-permute-start.4) | collective-permute-done | bytes 262176 | tf_op jit(solution)/shard_map/ppermute | solution.py:21
  32.6 0.0 collective-permute-start.6
  32.6 1.2 %collective-permute-start.1 = (f32[2,264,128]{2,1,0:T(8,128)S(1)}, f32[2,264,128]{2,1,0:T(8,128)S(1)}, u32[]{:S(2)}, u32[]{:S(2)}) collective-permute-start(f32[2,264,128]{2,1,0:T(8,128)S(1)} %collective-permute-done.pack), channel_id=1, source_target_pairs={{0,2},{2,0},{1,3},{3,1},{4,6},{6,4},{5,7},{7,5},{8,10},{10,8},{9,1... | collective-permute-start | bytes 811016 | tf_op jit(solution)/shard_map/ppermute | solution.py:21
  33.8 0.8 collective-permute-start.5
  34.6 5.7 %collective-permute-done.6.cross_a = f32[256,128]{1,0:T(8,128)S(1)} collective-permute-done((f32[256,128]{1,0:T(8,128)}, f32[256,128]{1,0:T(8,128)S(1)}, u32[]{:S(2)}, u32[]{:S(2)}) %collective-permute-start.6) | collective-permute-done | bytes 131104 | tf_op jit(solution)/shard_map/ppermute | solution.py:21
  40.3 0.0 collective-permute-start.7
  40.3 0.0 collective-permute-done.2.mate
  40.3 1.0 %collective-permute-start.8 = (f32[256,128]{1,0:T(8,128)S(1)}, f32[256,128]{1,0:T(8,128)S(1)}, u32[]{:S(2)}, u32[]{:S(2)}) collective-permute-start(f32[256,128]{1,0:T(8,128)S(1)} %collective-permute-done.6.cross_a), channel_id=1, source_target_pairs={{0,2},{2,0},{1,3},{3,1},{4,6},{6,4},{5,7},{7,5},{8,10},{10,8},{9,1... | collective-permute-start | bytes 393224 | tf_op jit(solution)/shard_map/ppermute | solution.py:21
  41.2 6.5 %collective-permute-done.7.cross_b = f32[256,128]{1,0:T(8,128)S(1)} collective-permute-done((f32[256,128]{1,0:T(8,128)}, f32[256,128]{1,0:T(8,128)S(1)}, u32[]{:S(2)}, u32[]{:S(2)}) %collective-permute-start.7) | collective-permute-done | bytes 131104 | tf_op jit(solution)/shard_map/ppermute | solution.py:21
  47.7 1.2 %collective-permute-start.9 = (f32[256,128]{1,0:T(8,128)S(1)}, f32[256,128]{1,0:T(8,128)S(1)}, u32[]{:S(2)}, u32[]{:S(2)}) collective-permute-start(f32[256,128]{1,0:T(8,128)S(1)} %collective-permute-done.7.cross_b), channel_id=1, source_target_pairs={{0,2},{2,0},{1,3},{3,1},{4,6},{6,4},{5,7},{7,5},{8,10},{10,8},{9,1... | collective-permute-start | bytes 393224 | tf_op jit(solution)/shard_map/ppermute | solution.py:21
  49.0 0.0 copy-start.1
  49.0 1.0 %copy-done.1 = f32[2,256,256]{2,1,0:T(8,128)S(1)} copy-done((f32[2,256,256]{2,1,0:T(8,128)S(1)}, f32[2,256,256]{2,1,0:T(8,128)}, u32[]{:S(2)}) %copy-start.1) | copy-done | bytes 524312
  50.0 8.6 %eliminate_y.1 = (f32[2,5,128,128]{3,2,1,0:T(8,128)S(1)}, f32[2,3,128,256]{3,2,1,0:T(8,128)S(1)}) custom-call(f32[2,264,128]{2,1,0:T(8,128)S(1)} %copy-done.2, f32[2,264,128]{2,1,0:T(8,128)S(1)} %collective-permute-done.2.mate, f32[2,256,256]{2,1,0:T(8,128)S(1)} %copy-done.1), custom_call_target="tpu_custom_call" | custom-call | flops 83886080 | bytes 1048576 | tf_op jit(solution)/shard_map/eliminate_y/pallas_call | solution.py:270
  58.6 8.8 %eliminate_x.1 = (f32[2,5,128,128]{3,2,1,0:T(8,128)S(1)}, f32[2,3,128,256]{3,2,1,0:T(8,128)S(1)}) custom-call(f32[2,264,128]{2,1,0:T(8,128)S(1)} %collective-permute-done.pack, f32[2,5,128,128]{3,2,1,0:T(8,128)S(1)} %get-tuple-element.17.one, f32[2,3,128,256]{3,2,1,0:T(8,128)S(1)} %get-tuple-element.18.sides_one), custom_call_target="tpu_custom_call" | custom-call | flops 83886080 | bytes 1048576 | tf_op jit(solution)/shard_map/eliminate_x/pallas_call | solution.py:270
  67.4 0.0 collective-permute-done.1.pack
  67.4 0.0 copy-start
  67.4 16.7 %eliminate_far.1.held = f32[2,4,128,256]{3,2,1,0:T(8,128)S(1)} custom-call(f32[2,264,128]{2,1,0:T(8,128)S(1)} %collective-permute-done.1.pack, f32[2,5,128,128]{3,2,1,0:T(8,128)S(1)} %get-tuple-element.17.one, f32[2,3,128,256]{3,2,1,0:T(8,128)S(1)} %get-tuple-element.18.sides_one, f32[2,5,128,128]{3,2,1,0:T(8,128)S(1)} %get-tuple-element.19.two, ...), custom_call_target="tpu_custom_call" | custom-call | flops 167772160 | bytes 1048576 | tf_op jit(solution)/shard_map/eliminate_far/pallas_call | solution.py:270
  84.2 0.0 collective-permute-done.3.mate
  84.2 0.0 collective-permute-done.5.far
  84.2 0.0 copy-done
  84.2 3.8 %near_columns.1.before = f32[2,256,1024]{2,1,0:T(8,128)} custom-call(f32[2,512,512]{2,1,0:T(8,128)S(1)} %bitcast.6, f32[2,4,128,256]{3,2,1,0:T(8,128)S(1)} %eliminate_far.1.held, f32[2,256,256]{2,1,0:T(8,128)S(1)} %copy-done.1, f32[2,256,256]{2,1,0:T(8,128)S(1)} %collective-permute-done.3.mate, f32[256,256]{1,0:T(8,128)S(1)} %collective-permute-done.4.cross, ...), custom_call_target="tpu_custom_call" | custom-call | flops 201326592 | bytes 1048576 | tf_op jit(solution)/shard_map/near_columns/pallas_call | solution.py:326
  88.1 0.0 collective-permute-done.8.far_a
  88.1 0.0 collective-permute-done.9.far_b
  88.1 1.8 %last_columns.1 = f32[2,256,1024]{2,1,0:T(8,128)} custom-call(f32[2,256,1024]{2,1,0:T(8,128)} %near_columns.1.before, f32[2,4,128,256]{3,2,1,0:T(8,128)S(1)} %eliminate_far.1.held, f32[256,128]{1,0:T(8,128)S(1)} %collective-permute-done.6.cross_a, f32[256,128]{1,0:T(8,128)S(1)} %collective-permute-done.7.cross_b, ...), custom_call_target="tpu_custom_call", output_to_operand_aliasing={{}: (0, {})} | custom-call | flops 67108864 | bytes 1048576 | tf_op jit(solution)/shard_map/last_columns/pallas_call | solution.py:368
Async XLA Ops:
  1.8 18.1 %copy-start.2 = (f32[2,264,128]{2,1,0:T(8,128)S(1)}, f32[2,264,128]{2,1,0:T(8,128)}, u32[]{:S(2)}) copy-start(f32[2,264,128]{2,1,0:T(8,128)} %interfaces.1.own) | copy-start | bytes 811012
  1.8 16.6 %collective-permute-start = (f32[2,264,128]{2,1,0:T(8,128)}, f32[2,264,128]{2,1,0:T(8,128)S(1)}, u32[]{:S(2)}, u32[]{:S(2)}) collective-permute-start(f32[2,264,128]{2,1,0:T(8,128)} %interfaces.1.own), channel_id=1, source_target_pairs={{0,8},{8,0},{4,12},{12,4},{1,9},{9,1},{5,13},{13,5},{2,10},{10,2},... | collective-permute-start | bytes 811016 | tf_op jit(solution)/shard_map/ppermute | solution.py:21
  18.4 14.2 %collective-permute-start.4 = (f32[256,256]{1,0:T(8,128)}, f32[256,256]{1,0:T(8,128)S(1)}, u32[]{:S(2)}, u32[]{:S(2)}) collective-permute-start(f32[256,256]{1,0:T(8,128)} %get-tuple-element.22), channel_id=1, source_target_pairs={{0,8},{8,0},{4,12},{12,4},{1,9},{9,1},{5,13},{13,5},{2,10},{10,2},... | collective-permute-start | bytes 786440 | tf_op jit(solution)/shard_map/ppermute | solution.py:21
  18.4 65.8 %collective-permute-start.3 = (f32[2,256,256]{2,1,0:T(8,128)}, f32[2,256,256]{2,1,0:T(8,128)S(1)}, u32[]{:S(2)}, u32[]{:S(2)}) collective-permute-start(f32[2,256,256]{2,1,0:T(8,128)} %get-tuple-element.16.coupling.own), channel_id=1, source_target_pairs={{0,2},{2,0},{1,3},{3,1},{4,6},{6,4},{5,7},{7,5},{8,10},{10,8},{9,1... | collective-permute-start | bytes 1572872 | tf_op jit(solution)/shard_map/ppermute | solution.py:21
  19.9 20.4 %collective-permute-start.2 = (f32[2,264,128]{2,1,0:T(8,128)S(1)}, f32[2,264,128]{2,1,0:T(8,128)S(1)}, u32[]{:S(2)}, u32[]{:S(2)}) collective-permute-start(f32[2,264,128]{2,1,0:T(8,128)S(1)} %copy-done.2), channel_id=1, source_target_pairs={{0,2},{2,0},{1,3},{3,1},{4,6},{6,4},{5,7},{7,5},{8,10},{10,8},{9,1... | collective-permute-start | bytes 811016 | tf_op jit(solution)/shard_map/ppermute | solution.py:21
  32.6 7.7 %collective-permute-start.6 = (f32[256,128]{1,0:T(8,128)}, f32[256,128]{1,0:T(8,128)S(1)}, u32[]{:S(2)}, u32[]{:S(2)}) collective-permute-start(f32[256,128]{1,0:T(8,128)} %get-tuple-element.24), channel_id=1, source_target_pairs={{0,8},{8,0},{4,12},{12,4},{1,9},{9,1},{5,13},{13,5},{2,10},{10,2},... | collective-permute-start | bytes 393224 | tf_op jit(solution)/shard_map/ppermute | solution.py:21
  32.6 34.8 %collective-permute-start.1 = (f32[2,264,128]{2,1,0:T(8,128)S(1)}, f32[2,264,128]{2,1,0:T(8,128)S(1)}, u32[]{:S(2)}, u32[]{:S(2)}) collective-permute-start(f32[2,264,128]{2,1,0:T(8,128)S(1)} %collective-permute-done.pack), channel_id=1, source_target_pairs={{0,2},{2,0},{1,3},{3,1},{4,6},{6,4},{5,7},{7,5},{8,10},{10,8},{9,1... | collective-permute-start | bytes 811016 | tf_op jit(solution)/shard_map/ppermute | solution.py:21
  33.8 50.4 %collective-permute-start.5 = (f32[256,256]{1,0:T(8,128)S(1)}, f32[256,256]{1,0:T(8,128)S(1)}, u32[]{:S(2)}, u32[]{:S(2)}) collective-permute-start(f32[256,256]{1,0:T(8,128)S(1)} %collective-permute-done.4.cross), channel_id=1, source_target_pairs={{0,2},{2,0},{1,3},{3,1},{4,6},{6,4},{5,7},{7,5},{8,10},{10,8},{9,1... | collective-permute-start | bytes 786440 | tf_op jit(solution)/shard_map/ppermute | solution.py:21
  40.3 7.5 %collective-permute-start.7 = (f32[256,128]{1,0:T(8,128)}, f32[256,128]{1,0:T(8,128)S(1)}, u32[]{:S(2)}, u32[]{:S(2)}) collective-permute-start(f32[256,128]{1,0:T(8,128)} %get-tuple-element.26), channel_id=1, source_target_pairs={{0,8},{8,0},{4,12},{12,4},{1,9},{9,1},{5,13},{13,5},{2,10},{10,2},... | collective-permute-start | bytes 393224 | tf_op jit(solution)/shard_map/ppermute | solution.py:21
  40.3 47.8 %collective-permute-start.8 = (f32[256,128]{1,0:T(8,128)S(1)}, f32[256,128]{1,0:T(8,128)S(1)}, u32[]{:S(2)}, u32[]{:S(2)}) collective-permute-start(f32[256,128]{1,0:T(8,128)S(1)} %collective-permute-done.6.cross_a), channel_id=1, source_target_pairs={{0,2},{2,0},{1,3},{3,1},{4,6},{6,4},{5,7},{7,5},{8,10},{10,8},{9,1... | collective-permute-start | bytes 393224 | tf_op jit(solution)/shard_map/ppermute | solution.py:21
  47.7 40.3 %collective-permute-start.9 = (f32[256,128]{1,0:T(8,128)S(1)}, f32[256,128]{1,0:T(8,128)S(1)}, u32[]{:S(2)}, u32[]{:S(2)}) collective-permute-start(f32[256,128]{1,0:T(8,128)S(1)} %collective-permute-done.7.cross_b), channel_id=1, source_target_pairs={{0,2},{2,0},{1,3},{3,1},{4,6},{6,4},{5,7},{7,5},{8,10},{10,8},{9,1... | collective-permute-start | bytes 393224 | tf_op jit(solution)/shard_map/ppermute | solution.py:21
  49.0 1.0 %copy-start.1 = (f32[2,256,256]{2,1,0:T(8,128)S(1)}, f32[2,256,256]{2,1,0:T(8,128)}, u32[]{:S(2)}) copy-start(f32[2,256,256]{2,1,0:T(8,128)} %get-tuple-element.16.coupling.own) | copy-start | bytes 1572868
  67.4 16.8 %copy-start = (f32[2,1,1,512,512]{4,3,2,1,0:T(8,128)S(1)}, f32[2,1,1,512,512]{4,3,2,1,0:T(8,128)}, u32[]{:S(2)}) copy-start(f32[2,1,1,512,512]{4,3,2,1,0:T(8,128)} %param.1) | copy-start | bytes 6291460

commit v2 on v1

--- a/solution.py
+++ b/solution.py
@@ -43,6 +43,10 @@
     )
 
 
+def work(microseconds):
+    return int(microseconds * 1e9)
+
+
 def tree(terms):
     while len(terms) > 1:
         terms = [terms[i] + terms[i + 1] for i in range(0, len(terms) - 1, 2)] + terms[len(terms) & ~1 :]
@@ -55,41 +59,47 @@
     many = len(matrices)
     lane = lax.broadcasted_iota(jnp.int32, (SUB, size), 1)
     sub = lax.broadcasted_iota(jnp.int32, (SUB, size), 0)
-    full = lambda v: jnp.broadcast_to(v, (SUB, size))
+
+    def full(v):
+        return jnp.broadcast_to(v, (SUB, size))
+
     state = [[m[SUB * i : SUB * i + SUB, :] for i in range(panels)] for m in matrices]
     lower = [[] for _ in matrices]
     scaled = [[] for _ in matrices]
     for p in range(panels):
         first = SUB * p
         inside = (lane >= first) & (lane < first + SUB)
-        unit = lane - first == sub
+        unit = jnp.where(lane - first == sub, 1.0, 0.0)
         done = lane < first + SUB
         blocks = [[full(state[w][p][:, first + j : first + j + 1]) for j in range(SUB)] for w in range(many)]
+        raw = [state[w][p] for w in range(many)]
+        panel = [jnp.where(inside, unit, raw[w]) for w in range(many)]
+        for w in range(many):
+            lower[w].append(jnp.where(done, panel[w], 0.0))
         for k in range(SUB):
             at_row = sub == k
             for w in range(many):
-                old = blocks[w]
-                pivot = old[k]
-                inverse = 1.0 / full(pivot[k : k + 1, :])
-                new = []
-                for j in range(SUB):
-                    if j == k:
-                        new.append(jnp.where(at_row, inverse, -pivot * inverse))
-                    else:
-                        scaled_row = full(old[j][k : k + 1, :]) * inverse
-                        new.append(jnp.where(at_row, scaled_row, old[j] - pivot * scaled_row))
-                blocks[w] = new
+                block = blocks[w]
+                inverse = 1.0 / full(block[k][k : k + 1])
+                factor = jnp.where(at_row, -1.0, block[k])
+
+                def step(x):
+                    return jnp.where(at_row, 0.0, x) - (factor * full(x[k : k + 1])) * inverse
+
+                for j in range(k + 1, SUB):
+                    block[j] = step(block[j])
+                panel[w] = step(panel[w])
         for w in range(many):
-            rows = state[w]
-            panel = jnp.where(inside, jnp.where(unit, 1.0, 0.0), rows[p])
-            gained = tree([blocks[w][l] * full(panel[l : l + 1, :]) for l in range(SUB)])
-            lower[w].append(jnp.where(done, panel, 0.0))
+            gained, rows = panel[w], state[w]
             scaled[w].append(jnp.where(done, gained, 0.0))
-            spread = [full(gained[l : l + 1, :]) for l in range(SUB)]
-            for i in range(p + 1, panels):
-                row = rows[i]
-                change = tree([full(row[:, first + l : first + l + 1]) * spread[l] for l in range(SUB)])
-                rows[i] = jnp.where(inside, 0.0, row) - change
+            if p + 2 < panels:
+                change = mul_t(raw[w], gained)
+                for i in range(p + 2, panels):
+                    rows[i] = jnp.where(inside, 0.0, rows[i]) - change[SUB * i : SUB * i + SUB]
+            if p + 1 < panels:
+                row = rows[p + 1]
+                terms = [full(row[:, first + l : first + l + 1]) * full(gained[l : l + 1]) for l in range(SUB)]
+                rows[p + 1] = jnp.where(inside, 0.0, row) - tree(terms)
     return [mul_t(jnp.concatenate(lower[w], 0), jnp.concatenate(scaled[w], 0)) for w in range(many)]
 
 
@@ -154,7 +164,7 @@
             pltpu.VMEM((waves, side, side), jnp.float32),
             pltpu.SemaphoreType.DMA((3 * waves,)),
         ],
-        cost_estimate=pl.CostEstimate(flops=0, bytes_accessed=5 * waves * side * side * 4, transcendentals=0),
+        cost_estimate=pl.CostEstimate(flops=work(1.5), bytes_accessed=5 * waves * side * side * 4, transcendentals=0),
     )(tiles)
 
 
@@ -194,75 +204,76 @@
         in_specs=[pl.BlockSpec(memory_space=pl.ANY)],
         out_specs=[pl.BlockSpec(memory_space=pltpu.VMEM)] * 4,
         scratch_shapes=[pltpu.SemaphoreType.DMA((8 * waves,))],
-        cost_estimate=pl.CostEstimate(flops=0, bytes_accessed=16 * waves * side * side * 4, transcendentals=0),
+        cost_estimate=pl.CostEstimate(flops=work(2), bytes_accessed=16 * waves * side * side * 4, transcendentals=0),
     )(tiles)
 
 
-def first_kernel(side, own, mate, coupling, blocks, sides):
+def first_kernel(side, own, mate, coupling, solved, rest):
     waves = own.shape[0]
-    sums = [pack_yy(own[w, 0:side, :] + mate[w, 0:side, :]) for w in range(waves)]
-    inverse = inverses(sums)
-    for w in range(waves):
-        own_yx = own[w, side : 2 * side, :]
-        mate_yu = mate[w, side : 2 * side, :]
-        gain_x = mul(inverse[w], own_yx)
-        gain_u = mul(inverse[w], mate_yu)
-        blocks[w, 0] = gain_x
-        blocks[w, 1] = gain_u
-        blocks[w, 2] = pack_xx(own[w, 0:side, :], own[w, 2 * side : 2 * side + 1, :]) - mul_t(own_yx, gain_x)
-        blocks[w, 3] = -mul_t(own_yx, gain_u)
-        blocks[w, 4] = pack_xx(mate[w, 0:side, :], mate[w, 2 * side : 2 * side + 1, :]) - mul_t(mate_yu, gain_u)
-        side_y = coupling[w, 0:side, :]
-        sides[w, 0] = mul(inverse[w], side_y)
-        sides[w, 1] = coupling[w, side:, :] - mul_t(gain_x, side_y)
-        sides[w, 2] = -mul_t(gain_u, side_y)
-
-
-def second_kernel(side, pack, one, sides_one, blocks, sides):
+    inverse = inverses([pack_yy(own[w, 0:side, :] + mate[w, 0:side, :]) for w in range(waves)])
+    for w in range(waves):
+        across = jnp.concatenate([own[w, side : 2 * side, :], mate[w, side : 2 * side, :]], 1)
+        gains = mul(inverse[w], jnp.concatenate([across, coupling[w, 0:side, :]], 1))
+        solved[w] = gains
+        change = mul_t(across, gains)
+        lines = own[w, 2 * side : 2 * side + 1, :], mate[w, 2 * side : 2 * side + 1, :]
+        rest[w, 0:side, 0:side] = pack_xx(own[w, 0:side, :], lines[0]) - change[0:side, 0:side]
+        rest[w, 0:side, side : 2 * side] = -change[0:side, side : 2 * side]
+        rest[w, 0:side, 2 * side :] = coupling[w, side:, :] - change[0:side, 2 * side :]
+        rest[w, side:, 0:side] = -change[side:, 0:side]
+        rest[w, side:, side : 2 * side] = pack_xx(mate[w, 0:side, :], lines[1]) - change[side:, side : 2 * side]
+        rest[w, side:, 2 * side :] = -change[side:, 2 * side :]
+
+
+def second_kernel(side, pack, solved_y, rest, solved, left):
     waves = pack.shape[0]
-    sums = [
-        one[w, 2] + pack_xx(pack[w, 0:side, :], pack[w, 2 * side : 2 * side + 1, :]) for w in range(waves)
-    ]
-    inverse = inverses(sums)
-    for w in range(waves):
-        vx = pack[w, side : 2 * side, :]
-        xu = one[w, 3]
-        gain_v = mul(inverse[w], vx.T)
-        gain_u = mul(inverse[w], xu)
-        blocks[w, 0] = gain_v
-        blocks[w, 1] = gain_u
-        blocks[w, 2] = pack_yy(pack[w, 0:side, :]) - mul(vx, gain_v)
-        blocks[w, 3] = -mul(vx, gain_u)
-        blocks[w, 4] = one[w, 4] - mul_t(xu, gain_u)
-        side_x = sides_one[w, 1]
-        sides[w, 0] = mul(inverse[w], side_x)
-        sides[w, 1] = -mul_t(gain_v, side_x)
-        sides[w, 2] = sides_one[w, 2] - mul_t(gain_u, side_x)
-
-
-def third_kernel(side, pack, one, sides_one, two, sides_two, held):
-    waves = pack.shape[0]
-    inverse_v = inverses([two[w, 2] + pack_yy(pack[w, 0:side, :]) for w in range(waves)])
-    vu = [two[w, 3] + pack[w, side : 2 * side, :] for w in range(waves)]
-    gain = [mul(inverse_v[w], vu[w]) for w in range(waves)]
-    inverse_u = inverses(
+    inverse = inverses(
         [
-            two[w, 4]
-            + pack_xx(pack[w, 0:side, :], pack[w, 2 * side : 2 * side + 1, :])
-            - mul_t(vu[w], gain[w])
+            rest[w, 0:side, 0:side] + pack_xx(pack[w, 0:side, :], pack[w, 2 * side : 2 * side + 1, :])
             for w in range(waves)
         ]
     )
     for w in range(waves):
-        side_v = sides_two[w, 1]
-        side_u = sides_two[w, 2] - mul_t(gain[w], side_v)
-        held_u = mul(inverse_u[w], side_u)
-        held_v = mul(inverse_v[w], side_v) - mul(gain[w], held_u)
-        held_x = sides_two[w, 0] - mul(two[w, 0], held_v) - mul(two[w, 1], held_u)
-        held_y = sides_one[w, 0] - mul(one[w, 0], held_x) - mul(one[w, 1], held_u)
-        held[w, 0] = held_y
-        held[w, 1] = held_x
-        held[w, 2] = held_v
+        vx = pack[w, side : 2 * side, :]
+        gains = mul(inverse[w], jnp.concatenate([vx.T, rest[w, 0:side, side:]], 1))
+        solved[w] = gains
+        column = jnp.concatenate([vx, rest[w, side:, 0:side], solved_y[w, :, 0:side]], 0)
+        change = mul(column, gains)
+        left[w, 0:side, 0:side] = pack_yy(pack[w, 0:side, :]) - change[0:side, 0:side]
+        left[w, 0:side, side:] = -change[0:side, side:]
+        left[w, side:, 0:side] = -change[side:, 0:side]
+        left[w, side : 2 * side, side:] = rest[w, side:, side:] - change[side : 2 * side, side:]
+        left[w, 2 * side :, side:] = solved_y[w, :, side:] - change[2 * side :, side:]
+
+
+def third_kernel(side, pack, solved_x, left, solved, last):
+    waves = pack.shape[0]
+    inverse = inverses([left[w, 0:side, 0:side] + pack_yy(pack[w, 0:side, :]) for w in range(waves)])
+    for w in range(waves):
+        vu = pack[w, side : 2 * side, :]
+        row = jnp.concatenate([left[w, 0:side, side : 2 * side] + vu, left[w, 0:side, 2 * side :]], 1)
+        gains = mul(inverse[w], row)
+        solved[w] = gains
+        column = jnp.concatenate(
+            [left[w, side : 2 * side, 0:side] + vu.T, left[w, 2 * side :, 0:side], solved_x[w, :, 0:side]], 0
+        )
+        change = mul(column, gains)
+        uu = pack_xx(pack[w, 0:side, :], pack[w, 2 * side : 2 * side + 1, :])
+        last[w, 0:side, 0:side] = left[w, side : 2 * side, side : 2 * side] + uu - change[0:side, 0:side]
+        last[w, 0:side, side:] = left[w, side : 2 * side, 2 * side :] - change[0:side, side:]
+        last[w, side : 2 * side, :] = left[w, 2 * side :, side:] - change[side : 2 * side, :]
+        last[w, 2 * side :, :] = solved_x[w, :, side:] - change[2 * side :, :]
+
+
+def fourth_kernel(side, solved_v, last, held):
+    waves = last.shape[0]
+    inverse = inverses([last[w, 0:side, 0:side] for w in range(waves)])
+    for w in range(waves):
+        held_u = mul(inverse[w], last[w, 0:side, side:])
+        change = mul(jnp.concatenate([last[w, side:, 0:side], solved_v[w, :, 0:side]], 0), held_u)
+        held[w, 0] = last[w, side : 2 * side, side:] - change[0:side]
+        held[w, 1] = last[w, 2 * side :, side:] - change[side : 2 * side]
+        held[w, 2] = solved_v[w, :, side:] - change[2 * side :]
         held[w, 3] = held_u
 
 
@@ -336,7 +347,7 @@
             pltpu.SemaphoreType.DMA((3 * waves,)),
         ],
         compiler_params=pltpu.CompilerParams(vmem_limit_bytes=32 << 20),
-        cost_estimate=pl.CostEstimate(flops=12 * (2 * side) ** 3, bytes_accessed=1 << 20, transcendentals=0),
+        cost_estimate=pl.CostEstimate(flops=work(4), bytes_accessed=1 << 20, transcendentals=0),
     )(tiles, held, own, mate, cross, far)
 
 
@@ -377,7 +388,7 @@
         ],
         input_output_aliases={0: 0},
         compiler_params=pltpu.CompilerParams(vmem_limit_bytes=32 << 20),
-        cost_estimate=pl.CostEstimate(flops=4 * (2 * side) ** 3, bytes_accessed=1 << 20, transcendentals=0),
+        cost_estimate=pl.CostEstimate(flops=work(2), bytes_accessed=1 << 20, transcendentals=0),
     )(before, held, *pieces)
 
 
@@ -388,29 +399,30 @@
     whole, *parts = couplings(tiles)
     mate_pack = swapped(pack, "gy")
     cross_pack = swapped(pack, "gx")
+    mate = swapped(whole, "gy")
+
+    def eliminate(kernel, name, shapes, time):
+        return whole_call(functools.partial(kernel, side), name, [(waves, *shape) for shape in shapes], work(time))
+
+    full = 4 * side
+    solved_y, rest = eliminate(first_kernel, "eliminate_y", [(side, full), (2 * side, full)], 7)(
+        pack, mate_pack, whole
+    )
+    cross_0 = swapped(after(parts[0], (cross_pack, solved_y)), "gx")
     far_pack = swapped(cross_pack, "gy")
-    mate = swapped(whole, "gy")
-    previous = cross_pack
-    cross = []
-    far = []
-    for part in parts:
-        previous = swapped(after(part, previous), "gx")
-        cross.append(previous)
-        far.append(swapped(previous, "gy"))
-    square = side * side
-    matrix, sides = (waves, 5, side, side), (waves, 3, side, 2 * side)
-    one, sides_one = whole_call(
-        functools.partial(first_kernel, side), "eliminate_y", [matrix, sides], 20 * waves * square * side
-    )(pack, mate_pack, whole)
-    two, sides_two = whole_call(
-        functools.partial(second_kernel, side), "eliminate_x", [matrix, sides], 20 * waves * square * side
-    )(cross_pack, one, sides_one)
-    (held,) = whole_call(
-        functools.partial(third_kernel, side),
-        "eliminate_far",
-        [(waves, 4, side, 2 * side)],
-        40 * waves * square * side,
-    )(far_pack, one, sides_one, two, sides_two)
+    solved_x, left = eliminate(second_kernel, "eliminate_x", [(side, full), (3 * side, full)], 7)(
+        cross_pack, solved_y, rest
+    )
+    cross_1 = swapped(after(parts[1], (cross_0, solved_x)), "gx")
+    solved_v, last = eliminate(third_kernel, "eliminate_v", [(side, 3 * side), (3 * side, 3 * side)], 7)(
+        far_pack, solved_x, left
+    )
+    far_0 = swapped(cross_0, "gy")
+    cross_2 = swapped(after(parts[2], (cross_1, solved_v)), "gx")
+    far_1 = swapped(cross_1, "gy")
+    (held,) = eliminate(fourth_kernel, "eliminate_u", [(4, side, 2 * side)], 7)(solved_v, last)
+    far_2 = swapped(cross_2, "gy")
+    cross, far = (cross_0, cross_1, cross_2), (far_0, far_1, far_2)
     near = near_call(tiles, held, whole, mate, cross[0], far[0])
     merged = last_call(near, held, cross[1], cross[2], far[1], far[2])
     return merged[:, None, None]

time: 90.3 us -> 60.6 us (0.67)
  waiting for transfers between devices: 34.5 us -> 1.97 us
  starting transfers between devices: 10.4 us -> 18.4 us
  Pallas kernels: 43.8 us -> 38.7 us
    ppermute x10, waiting for transfers between devices: 34.5 us -> 1.97 us  [swapped(): return lax.ppermute(block, axis, route)]
    ppermute x10, starting transfers between devices: 10.4 us -> 18.4 us  [swapped(): return lax.ppermute(block, axis, route)]
    pallas_call x3 -> x4, Pallas kernels: 34.1 us -> 28.7 us  [whole_call(): pl.pallas_call(kernel, name=name, out_shape=[jax.ShapeDtypeStruct(s, jnp....]
  transfers between devices with their start and end apart: 10 -> 10, of which waited for: 4 -> 3; matrix products, arithmetic and copies ran while one was open for 0% -> 0% of each run, Pallas kernels for 45% -> 58%
where the time goes in v2:
time: 60.6 us; the launch traced here: 60.4 us
  Pallas kernels  38.7 us (64%)
  starting transfers between devices  18.4 us (30%)
  waiting for transfers between devices  1.97 us (3%)
  local copies, waits for them, and re-layouts  1.06 us (2%)
    pallas_call x4, Pallas kernels, whole_call(): pl.pallas_call(kernel, name=name, out_shape=[jax.ShapeDtypeStruct(s, jnp....  28.7 us
    ppermute x10, starting transfers between devices, swapped(): return lax.ppermute(block, axis, route)  18.4 us
    pallas_call x1, Pallas kernels, near_call(): pl.pallas_call(functools.partial(near_kernel, side), name='near_columns',...  4.03 us
    pallas_call x1, Pallas kernels, couplings(): pl.pallas_call(functools.partial(coupling_kernel, side), name='couplings'...  2.36 us
    ppermute x10, waiting for transfers between devices, swapped(): return lax.ppermute(block, axis, route)  1.97 us
    pallas_call x1, Pallas kernels, last_call(): pl.pallas_call(functools.partial(last_kernel, side), name='last_columns',...  1.77 us
    pallas_call x1, Pallas kernels, interfaces(): pl.pallas_call(functools.partial(interface_kernel, side), name='interface...  1.77 us
  transfers between devices with their start and end apart: 10, of which 3 were waited for; matrix products, arithmetic and copies ran while one was open for 0% of the time, Pallas kernels for 58%

profile of v2, /device:TPU:0, one launch (start us, length us, event | category | flops | bytes accessed | tf_op | source)
XLA Modules:
  0.0 60.4 jit_solution(18233643722694061661)
XLA Ops:
  0.0 1.8 %interfaces.1.own = f32[2,264,128]{2,1,0:T(8,128)} custom-call(f32[2,512,512]{2,1,0:T(8,128)} %bitcast.4), custom_call_target="tpu_custom_call" | custom-call | flops 1500000000 | bytes 655360 | tf_op jit(solution)/shard_map/interfaces/pallas_call | solution.py:156
  1.8 0.0 copy-start.3
  1.8 3.0 %collective-permute-start.2 = (f32[2,264,128]{2,1,0:T(8,128)}, f32[2,264,128]{2,1,0:T(8,128)S(1)}, u32[]{:S(2)}, u32[]{:S(2)}) collective-permute-start(f32[2,264,128]{2,1,0:T(8,128)} %interfaces.1.own), channel_id=1, source_target_pairs={{0,2},{2,0},{1,3},{3,1},{4,6},{6,4},{5,7},{7,5},{8,10},{10,8},{9,1... | collective-permute-start | bytes 811016 | tf_op jit(solution)/shard_map/ppermute | solution.py:21
  4.8 2.6 %collective-permute-start = (f32[2,264,128]{2,1,0:T(8,128)}, f32[2,264,128]{2,1,0:T(8,128)S(1)}, u32[]{:S(2)}, u32[]{:S(2)}) collective-permute-start(f32[2,264,128]{2,1,0:T(8,128)} %interfaces.1.own), channel_id=1, source_target_pairs={{0,8},{8,0},{4,12},{12,4},{1,9},{9,1},{5,13},{13,5},{2,10},{10,2},... | collective-permute-start | bytes 811016 | tf_op jit(solution)/shard_map/ppermute | solution.py:21
  7.4 2.4 %couplings.1 = (f32[2,256,256]{2,1,0:T(8,128)}, f32[256,256]{1,0:T(8,128)}, f32[256,128]{1,0:T(8,128)}, f32[256,128]{1,0:T(8,128)}) custom-call(f32[2,512,512]{2,1,0:T(8,128)} %bitcast.5), custom_call_target="tpu_custom_call" | custom-call | flops 2000000000 | bytes 2097152 | tf_op jit(solution)/shard_map/couplings/pallas_call | solution.py:200
  9.7 0.7 %collective-permute-start.3 = (f32[2,256,256]{2,1,0:T(8,128)}, f32[2,256,256]{2,1,0:T(8,128)S(1)}, u32[]{:S(2)}, u32[]{:S(2)}) collective-permute-start(f32[2,256,256]{2,1,0:T(8,128)} %get-tuple-element.18.coupling.own), channel_id=1, source_target_pairs={{0,2},{2,0},{1,3},{3,1},{4,6},{6,4},{5,7},{7,5},{8,10},{10,8},{9,1... | collective-permute-start | bytes 1572872 | tf_op jit(solution)/shard_map/ppermute | solution.py:21
  10.5 1.0 %collective-permute-done.2.mate = f32[2,264,128]{2,1,0:T(8,128)S(1)} collective-permute-done((f32[2,264,128]{2,1,0:T(8,128)}, f32[2,264,128]{2,1,0:T(8,128)S(1)}, u32[]{:S(2)}, u32[]{:S(2)}) %collective-permute-start.2) | collective-permute-done | bytes 270368 | tf_op jit(solution)/shard_map/ppermute | solution.py:21
  11.5 0.0 copy-done.3
  11.5 0.0 copy-start.1
  11.5 1.0 %copy-done.1 = f32[2,256,256]{2,1,0:T(8,128)S(1)} copy-done((f32[2,256,256]{2,1,0:T(8,128)S(1)}, f32[2,256,256]{2,1,0:T(8,128)}, u32[]{:S(2)}) %copy-start.1) | copy-done | bytes 524312
  12.5 0.0 copy-start.4
  12.5 7.4 %eliminate_y.1 = (f32[2,128,512]{2,1,0:T(8,128)S(1)}, f32[2,256,512]{2,1,0:T(8,128)S(1)}) custom-call(f32[2,264,128]{2,1,0:T(8,128)S(1)} %copy-done.3, f32[2,264,128]{2,1,0:T(8,128)S(1)} %collective-permute-done.2.mate, f32[2,256,256]{2,1,0:T(8,128)S(1)} %copy-done.1), custom_call_target="tpu_custom_call" | custom-call | flops 7000000000 | bytes 1048576 | tf_op jit(solution)/shard_map/eliminate_y/pallas_call | solution.py:281
  20.0 0.0 collective-permute-done.pack
  20.0 0.0 copy-done.4
  20.0 4.0 %collective-permute-start.4 = (f32[256,256]{1,0:T(8,128)S(1)}, f32[256,256]{1,0:T(8,128)S(1)}, u32[]{:S(2)}, u32[]{:S(2)}) collective-permute-start(f32[256,256]{1,0:T(8,128)S(1)} %copy-done.4), channel_id=1, source_target_pairs={{0,8},{8,0},{4,12},{12,4},{1,9},{9,1},{5,13},{13,5},{2,10},{10,2},... | collective-permute-start | bytes 786440 | tf_op jit(solution)/shard_map/ppermute | solution.py:21
  24.0 1.5 %collective-permute-start.1 = (f32[2,264,128]{2,1,0:T(8,128)S(1)}, f32[2,264,128]{2,1,0:T(8,128)S(1)}, u32[]{:S(2)}, u32[]{:S(2)}) collective-permute-start(f32[2,264,128]{2,1,0:T(8,128)S(1)} %collective-permute-done.pack), channel_id=1, source_target_pairs={{0,2},{2,0},{1,3},{3,1},{4,6},{6,4},{5,7},{7,5},{8,10},{10,8},{9,1... | collective-permute-start | bytes 811016 | tf_op jit(solution)/shard_map/ppermute | solution.py:21
  25.5 0.0 copy-start.6
  25.5 7.8 %eliminate_x.1 = (f32[2,128,512]{2,1,0:T(8,128)S(1)}, f32[2,384,512]{2,1,0:T(8,128)S(1)}) custom-call(f32[2,264,128]{2,1,0:T(8,128)S(1)} %collective-permute-done.pack, f32[2,128,512]{2,1,0:T(8,128)S(1)} %get-tuple-element.19.solved_y, f32[2,256,512]{2,1,0:T(8,128)S(1)} %get-tuple-element.20.rest), custom_call_target="tpu_custom_call" | custom-call | flops 7000000000 | bytes 1048576 | tf_op jit(solution)/shard_map/eliminate_x/pallas_call | solution.py:281
  33.4 0.7 %collective-permute-done.4.cross = f32[256,256]{1,0:T(8,128)S(1)} collective-permute-done((f32[256,256]{1,0:T(8,128)S(1)}, f32[256,256]{1,0:T(8,128)S(1)}, u32[]{:S(2)}, u32[]{:S(2)}) %collective-permute-start.4) | collective-permute-done | bytes 262176 | tf_op jit(solution)/shard_map/ppermute | solution.py:21
  34.1 0.0 copy-done.6
  34.1 0.0 collective-permute-start.6
  34.1 1.4 %collective-permute-start.5 = (f32[256,256]{1,0:T(8,128)S(1)}, f32[256,256]{1,0:T(8,128)S(1)}, u32[]{:S(2)}, u32[]{:S(2)}) collective-permute-start(f32[256,256]{1,0:T(8,128)S(1)} %collective-permute-done.4.cross), channel_id=1, source_target_pairs={{0,2},{2,0},{1,3},{3,1},{4,6},{6,4},{5,7},{7,5},{8,10},{10,8},{9,1... | collective-permute-start | bytes 786440 | tf_op jit(solution)/shard_map/ppermute | solution.py:21
  35.5 0.0 collective-permute-done.1.pack
  35.5 0.0 copy-start.5
  35.5 7.1 %eliminate_v.1 = (f32[2,128,384]{2,1,0:T(8,128)S(1)}, f32[2,384,384]{2,1,0:T(8,128)S(1)}) custom-call(f32[2,264,128]{2,1,0:T(8,128)S(1)} %collective-permute-done.1.pack, f32[2,128,512]{2,1,0:T(8,128)S(1)} %get-tuple-element.21.solved_x, f32[2,384,512]{2,1,0:T(8,128)S(1)} %get-tuple-element.22.left), custom_call_target="tpu_custom_call" | custom-call | flops 7000000000 | bytes 1048576 | tf_op jit(solution)/shard_map/eliminate_v/pallas_call | solution.py:281
  42.6 0.0 collective-permute-done.6.cross_a
  42.6 0.0 copy-done.5
  42.7 3.0 %collective-permute-start.7 = (f32[256,128]{1,0:T(8,128)S(1)}, f32[256,128]{1,0:T(8,128)S(1)}, u32[]{:S(2)}, u32[]{:S(2)}) collective-permute-start(f32[256,128]{1,0:T(8,128)S(1)} %copy-done.5), channel_id=1, source_target_pairs={{0,8},{8,0},{4,12},{12,4},{1,9},{9,1},{5,13},{13,5},{2,10},{10,2},... | collective-permute-start | bytes 393224 | tf_op jit(solution)/shard_map/ppermute | solution.py:21
  45.6 0.0 copy-start
  45.6 0.0 copy-start.2
  45.6 6.3 %eliminate_u.1.held = f32[2,4,128,256]{3,2,1,0:T(8,128)S(1)} custom-call(f32[2,128,384]{2,1,0:T(8,128)S(1)} %get-tuple-element.23.solved_v, f32[2,384,384]{2,1,0:T(8,128)S(1)} %get-tuple-element.24.last), custom_call_target="tpu_custom_call" | custom-call | flops 7000000000 | bytes 1048576 | tf_op jit(solution)/shard_map/eliminate_u/pallas_call | solution.py:281
  52.0 0.7 %collective-permute-start.8 = (f32[256,128]{1,0:T(8,128)S(1)}, f32[256,128]{1,0:T(8,128)S(1)}, u32[]{:S(2)}, u32[]{:S(2)}) collective-permute-start(f32[256,128]{1,0:T(8,128)S(1)} %collective-permute-done.6.cross_a), channel_id=1, source_target_pairs={{0,2},{2,0},{1,3},{3,1},{4,6},{6,4},{5,7},{7,5},{8,10},{10,8},{9,1... | collective-permute-start | bytes 393224 | tf_op jit(solution)/shard_map/ppermute | solution.py:21
  52.7 0.0 collective-permute-done.7.cross_b
  52.7 1.4 %collective-permute-start.9 = (f32[256,128]{1,0:T(8,128)S(1)}, f32[256,128]{1,0:T(8,128)S(1)}, u32[]{:S(2)}, u32[]{:S(2)}) collective-permute-start(f32[256,128]{1,0:T(8,128)S(1)} %collective-permute-done.7.cross_b), channel_id=1, source_target_pairs={{0,2},{2,0},{1,3},{3,1},{4,6},{6,4},{5,7},{7,5},{8,10},{10,8},{9,1... | collective-permute-start | bytes 393224 | tf_op jit(solution)/shard_map/ppermute | solution.py:21
  54.1 0.0 collective-permute-done.3.mate
  54.1 0.0 collective-permute-done.5.far
  54.1 0.0 copy-done
  54.1 0.0 copy-done.2
  54.1 4.0 %near_columns.1.before = f32[2,256,1024]{2,1,0:T(8,128)} custom-call(f32[2,512,512]{2,1,0:T(8,128)S(1)} %bitcast.6, f32[2,4,128,256]{3,2,1,0:T(8,128)S(1)} %eliminate_u.1.held, f32[2,256,256]{2,1,0:T(8,128)S(1)} %copy-done.2, f32[2,256,256]{2,1,0:T(8,128)S(1)} %collective-permute-done.3.mate, f32[256,256]{1,0:T(8,128)S(1)} %collective-permute-done.4.cross, ...), custom_call_target="tpu_custom_call" | custom-call | flops 4000000000 | bytes 1048576 | tf_op jit(solution)/shard_map/near_columns/pallas_call | solution.py:337
  58.1 0.0 collective-permute-done.8.far_a
  58.1 0.3 collective-permute-done.9.far_b
  58.4 1.8 %last_columns.1 = f32[2,256,1024]{2,1,0:T(8,128)} custom-call(f32[2,256,1024]{2,1,0:T(8,128)} %near_columns.1.before, f32[2,4,128,256]{3,2,1,0:T(8,128)S(1)} %eliminate_u.1.held, f32[256,128]{1,0:T(8,128)S(1)} %collective-permute-done.6.cross_a, f32[256,128]{1,0:T(8,128)S(1)} %collective-permute-done.7.cross_b, ...), custom_call_target="tpu_custom_call", output_to_operand_aliasing={{}: (0, {})} | custom-call | flops 2000000000 | bytes 1048576 | tf_op jit(solution)/shard_map/last_columns/pallas_call | solution.py:379
Async XLA Ops:
  1.8 9.7 %copy-start.3 = (f32[2,264,128]{2,1,0:T(8,128)S(1)}, f32[2,264,128]{2,1,0:T(8,128)}, u32[]{:S(2)}) copy-start(f32[2,264,128]{2,1,0:T(8,128)} %interfaces.1.own) | copy-start | bytes 811012
  1.8 9.7 %collective-permute-start.2 = (f32[2,264,128]{2,1,0:T(8,128)}, f32[2,264,128]{2,1,0:T(8,128)S(1)}, u32[]{:S(2)}, u32[]{:S(2)}) collective-permute-start(f32[2,264,128]{2,1,0:T(8,128)} %interfaces.1.own), channel_id=1, source_target_pairs={{0,2},{2,0},{1,3},{3,1},{4,6},{6,4},{5,7},{7,5},{8,10},{10,8},{9,1... | collective-permute-start | bytes 811016 | tf_op jit(solution)/shard_map/ppermute | solution.py:21
  4.8 15.2 %collective-permute-start = (f32[2,264,128]{2,1,0:T(8,128)}, f32[2,264,128]{2,1,0:T(8,128)S(1)}, u32[]{:S(2)}, u32[]{:S(2)}) collective-permute-start(f32[2,264,128]{2,1,0:T(8,128)} %interfaces.1.own), channel_id=1, source_target_pairs={{0,8},{8,0},{4,12},{12,4},{1,9},{9,1},{5,13},{13,5},{2,10},{10,2},... | collective-permute-start | bytes 811016 | tf_op jit(solution)/shard_map/ppermute | solution.py:21
  9.7 44.3 %collective-permute-start.3 = (f32[2,256,256]{2,1,0:T(8,128)}, f32[2,256,256]{2,1,0:T(8,128)S(1)}, u32[]{:S(2)}, u32[]{:S(2)}) collective-permute-start(f32[2,256,256]{2,1,0:T(8,128)} %get-tuple-element.18.coupling.own), channel_id=1, source_target_pairs={{0,2},{2,0},{1,3},{3,1},{4,6},{6,4},{5,7},{7,5},{8,10},{10,8},{9,1... | collective-permute-start | bytes 1572872 | tf_op jit(solution)/shard_map/ppermute | solution.py:21
  11.5 1.0 %copy-start.1 = (f32[2,256,256]{2,1,0:T(8,128)S(1)}, f32[2,256,256]{2,1,0:T(8,128)}, u32[]{:S(2)}) copy-start(f32[2,256,256]{2,1,0:T(8,128)} %get-tuple-element.18.coupling.own) | copy-start | bytes 1572868
  12.5 7.4 %copy-start.4 = (f32[256,256]{1,0:T(8,128)S(1)}, f32[256,256]{1,0:T(8,128)}, u32[]{:S(2)}) copy-start(f32[256,256]{1,0:T(8,128)} %get-tuple-element.26) | copy-start | bytes 786436
  20.0 14.1 %collective-permute-start.4 = (f32[256,256]{1,0:T(8,128)S(1)}, f32[256,256]{1,0:T(8,128)S(1)}, u32[]{:S(2)}, u32[]{:S(2)}) collective-permute-start(f32[256,256]{1,0:T(8,128)S(1)} %copy-done.4), channel_id=1, source_target_pairs={{0,8},{8,0},{4,12},{12,4},{1,9},{9,1},{5,13},{13,5},{2,10},{10,2},... | collective-permute-start | bytes 786440 | tf_op jit(solution)/shard_map/ppermute | solution.py:21
  24.0 11.5 %collective-permute-start.1 = (f32[2,264,128]{2,1,0:T(8,128)S(1)}, f32[2,264,128]{2,1,0:T(8,128)S(1)}, u32[]{:S(2)}, u32[]{:S(2)}) collective-permute-start(f32[2,264,128]{2,1,0:T(8,128)S(1)} %collective-permute-done.pack), channel_id=1, source_target_pairs={{0,2},{2,0},{1,3},{3,1},{4,6},{6,4},{5,7},{7,5},{8,10},{10,8},{9,1... | collective-permute-start | bytes 811016 | tf_op jit(solution)/shard_map/ppermute | solution.py:21
  25.5 8.5 %copy-start.6 = (f32[256,128]{1,0:T(8,128)S(1)}, f32[256,128]{1,0:T(8,128)}, u32[]{:S(2)}) copy-start(f32[256,128]{1,0:T(8,128)} %get-tuple-element.28) | copy-start | bytes 393220
  34.1 8.6 %collective-permute-start.6 = (f32[256,128]{1,0:T(8,128)S(1)}, f32[256,128]{1,0:T(8,128)S(1)}, u32[]{:S(2)}, u32[]{:S(2)}) collective-permute-start(f32[256,128]{1,0:T(8,128)S(1)} %copy-done.6), channel_id=1, source_target_pairs={{0,8},{8,0},{4,12},{12,4},{1,9},{9,1},{5,13},{13,5},{2,10},{10,2},... | collective-permute-start | bytes 393224 | tf_op jit(solution)/shard_map/ppermute | solution.py:21
  34.1 20.0 %collective-permute-start.5 = (f32[256,256]{1,0:T(8,128)S(1)}, f32[256,256]{1,0:T(8,128)S(1)}, u32[]{:S(2)}, u32[]{:S(2)}) collective-permute-start(f32[256,256]{1,0:T(8,128)S(1)} %collective-permute-done.4.cross), channel_id=1, source_target_pairs={{0,2},{2,0},{1,3},{3,1},{4,6},{6,4},{5,7},{7,5},{8,10},{10,8},{9,1... | collective-permute-start | bytes 786440 | tf_op jit(solution)/shard_map/ppermute | solution.py:21
  35.5 7.2 %copy-start.5 = (f32[256,128]{1,0:T(8,128)S(1)}, f32[256,128]{1,0:T(8,128)}, u32[]{:S(2)}) copy-start(f32[256,128]{1,0:T(8,128)} %get-tuple-element.30) | copy-start | bytes 393220
  42.7 10.0 %collective-permute-start.7 = (f32[256,128]{1,0:T(8,128)S(1)}, f32[256,128]{1,0:T(8,128)S(1)}, u32[]{:S(2)}, u32[]{:S(2)}) collective-permute-start(f32[256,128]{1,0:T(8,128)S(1)} %copy-done.5), channel_id=1, source_target_pairs={{0,8},{8,0},{4,12},{12,4},{1,9},{9,1},{5,13},{13,5},{2,10},{10,2},... | collective-permute-start | bytes 393224 | tf_op jit(solution)/shard_map/ppermute | solution.py:21
  45.6 8.4 %copy-start = (f32[2,1,1,512,512]{4,3,2,1,0:T(8,128)S(1)}, f32[2,1,1,512,512]{4,3,2,1,0:T(8,128)}, u32[]{:S(2)}) copy-start(f32[2,1,1,512,512]{4,3,2,1,0:T(8,128)} %param.1) | copy-start | bytes 6291460
  45.6 8.4 %copy-start.2 = (f32[2,256,256]{2,1,0:T(8,128)S(1)}, f32[2,256,256]{2,1,0:T(8,128)}, u32[]{:S(2)}) copy-start(f32[2,256,256]{2,1,0:T(8,128)} %get-tuple-element.18.coupling.own) | copy-start | bytes 1572868
  52.0 6.2 %collective-permute-start.8 = (f32[256,128]{1,0:T(8,128)S(1)}, f32[256,128]{1,0:T(8,128)S(1)}, u32[]{:S(2)}, u32[]{:S(2)}) collective-permute-start(f32[256,128]{1,0:T(8,128)S(1)} %collective-permute-done.6.cross_a), channel_id=1, source_target_pairs={{0,2},{2,0},{1,3},{3,1},{4,6},{6,4},{5,7},{7,5},{8,10},{10,8},{9,1... | collective-permute-start | bytes 393224 | tf_op jit(solution)/shard_map/ppermute | solution.py:21
  52.7 5.8 %collective-permute-start.9 = (f32[256,128]{1,0:T(8,128)S(1)}, f32[256,128]{1,0:T(8,128)S(1)}, u32[]{:S(2)}, u32[]{:S(2)}) collective-permute-start(f32[256,128]{1,0:T(8,128)S(1)} %collective-permute-done.7.cross_b), channel_id=1, source_target_pairs={{0,2},{2,0},{1,3},{3,1},{4,6},{6,4},{5,7},{7,5},{8,10},{10,8},{9,1... | collective-permute-start | bytes 393224 | tf_op jit(solution)/shard_map/ppermute | solution.py:21

commit v3 on v2

v3 whole, which is shorter than its diff:
```python
import functools

import jax
import jax.numpy as jnp
from jax import lax
from jax.experimental import pallas as pl
from jax.experimental.pallas import tpu as pltpu
from jax.sharding import PartitionSpec as P

SUB = 8


def swapped(block, axis):
    count = lax.axis_size(axis)
    bit = count.bit_length() - 2
    route = []
    for low in range(count):
        high = low | 1 << bit
        if high != low and high < count:
            route += [(low, high), (high, low)]
    return lax.ppermute(block, axis, route)


def after(block, other):
    return lax.optimization_barrier((block, other))[0]


def role():
    right = (lax.axis_index("gx") >= lax.axis_size("gx") // 2).astype(jnp.int32)
    top = (lax.axis_index("gy") >= lax.axis_size("gy") // 2).astype(jnp.int32)
    return right, top


def mul(a, b):
    return lax.dot_general(
        a, b, (((1,), (0,)), ((), ())), precision=lax.Precision.HIGHEST, preferred_element_type=jnp.float32
    )


def mul_t(a, b):
    return lax.dot_general(
        a, b, (((0,), (0,)), ((), ())), precision=lax.Precision.HIGHEST, preferred_element_type=jnp.float32
    )


def work(microseconds):
    return int(microseconds * 1e9)


def tree(terms):
    while len(terms) > 1:
        terms = [terms[i] + terms[i + 1] for i in range(0, len(terms) - 1, 2)] + terms[len(terms) & ~1 :]
    return terms[0]


def inverses(matrices):
    size = matrices[0].shape[0]
    panels = size // SUB
    many = len(matrices)
    lane = lax.broadcasted_iota(jnp.int32, (SUB, size), 1)
    sub = lax.broadcasted_iota(jnp.int32, (SUB, size), 0)

    def full(v):
        return jnp.broadcast_to(v, (SUB, size))

    state = [[m[SUB * i : SUB * i + SUB, :] for i in range(panels)] for m in matrices]
    lower = [[] for _ in matrices]
    scaled = [[] for _ in matrices]
    for p in range(panels):
        first = SUB * p
        inside = (lane >= first) & (lane < first + SUB)
        unit = jnp.where(lane - first == sub, 1.0, 0.0)
        done = lane < first + SUB
        blocks = [[full(state[w][p][:, first + j : first + j + 1]) for j in range(SUB)] for w in range(many)]
        panel = [jnp.where(inside, unit, state[w][p]) for w in range(many)]
        for w in range(many):
            lower[w].append(jnp.where(done, panel[w], 0.0))
        for k in range(SUB):
            at_row = sub == k
            for w in range(many):
                block = blocks[w]
                inverse = 1.0 / full(block[k][k : k + 1])
                factor = jnp.where(at_row, -1.0, block[k])

                def step(x):
                    return jnp.where(at_row, 0.0, x) - (factor * full(x[k : k + 1])) * inverse

                for j in range(k + 1, SUB):
                    block[j] = step(block[j])
                panel[w] = step(panel[w])
        for w in range(many):
            gained, rows = panel[w], state[w]
            scaled[w].append(jnp.where(done, gained, 0.0))
            if p + 2 < panels:
                below = jnp.concatenate(rows[p + 2 :], 0)
                within = jnp.concatenate([inside] * (panels - p - 2), 0)
                empty = jnp.zeros((SUB, size), jnp.float32)
                placed = jnp.concatenate([gained if i == p else empty for i in range(panels)], 0)
                change = mul(jnp.where(within, below, 0.0), placed)
                for i in range(p + 2, panels):
                    at = SUB * (i - p - 2)
                    rows[i] = jnp.where(inside, 0.0, rows[i]) - change[at : at + SUB]
            if p + 1 < panels:
                row = rows[p + 1]
                terms = [full(row[:, first + l : first + l + 1]) * full(gained[l : l + 1]) for l in range(SUB)]
                rows[p + 1] = jnp.where(inside, 0.0, row) - tree(terms)
    return [mul_t(jnp.concatenate(lower[w], 0), jnp.concatenate(scaled[w], 0)) for w in range(many)]


def square_masks(side):
    row = lax.broadcasted_iota(jnp.int32, (side, side), 0)
    col = lax.broadcasted_iota(jnp.int32, (side, side), 1)
    return row > col, row == col


def pack_yy(square):
    below, diag = square_masks(square.shape[0])
    return jnp.where(below | diag, square, square.T)


def pack_xx(square, line):
    below, diag = square_masks(square.shape[0])
    return jnp.where(diag, jnp.broadcast_to(line, square.shape), jnp.where(below, square.T, square))


def block_of(tiles, side, w, row_side, col_side):
    rows = pl.ds(pl.multiple_of(row_side * side, side), side)
    cols = pl.ds(pl.multiple_of(col_side * side, side), side)
    return tiles.at[w, rows, cols]


def height(side):
    return 2 * side + SUB


def pack_kernel(side, units, tiles, own, sent, own_yy, own_xx, own_yx, sems, unit_sems):
    right, top = role()
    inner, outer = (3 - top, 1 - right), (right, 2 + top)
    waves = own_yy.shape[0]
    tall = height(side)
    copies = []
    for w in range(waves):
        for n, (i, j, target) in enumerate(((0, 0, own_yy), (1, 1, own_xx), (0, 1, own_yx))):
            source = block_of(tiles, side, w, inner[i], inner[j])
            copies.append(pltpu.make_async_copy(source, target.at[w], sems.at[3 * w + n]))
            copies[-1].start()
    others = load_units(tiles, side, inner, outer, units, sent, waves * tall, unit_sems, 0)
    below, diag = square_masks(side)
    for w in range(waves):
        for copy in copies[3 * w : 3 * w + 3]:
            copy.wait()
        xx = own_xx[w]
        square = jnp.where(below | diag, own_yy[w], xx)
        line = jnp.broadcast_to(jnp.sum(jnp.where(diag, xx, 0.0), 0, keepdims=True), (SUB, side))
        for target in (own, sent):
            target[w * tall : w * tall + side, :] = square
            target[w * tall + side : w * tall + 2 * side, :] = own_yx[w]
            target[w * tall + 2 * side : (w + 1) * tall, :] = line
    for copy in others:
        copy.wait()


def load_units(tiles, side, inner, outer, units, target, base, sems, first):
    copies = []
    for n, unit in enumerate(units):
        w, j = divmod(unit, 2)
        for i in range(2):
            place = target.at[pl.ds(base + (2 * n + i) * side, side), :]
            source = block_of(tiles, side, w, inner[i], outer[j])
            copies.append(pltpu.make_async_copy(source, place, sems.at[first + len(copies)]))
            copies[-1].start()
    return copies


def packed(tiles, units):
    waves, side = tiles.shape[0], tiles.shape[1] // 4
    square = pltpu.VMEM((waves, side, side), jnp.float32)
    rows = waves * height(side)
    return pl.pallas_call(
        functools.partial(pack_kernel, side, units),
        name="pack",
        out_shape=[
            jax.ShapeDtypeStruct((rows, side), jnp.float32),
            jax.ShapeDtypeStruct((rows + len(units) * 2 * side, side), jnp.float32),
        ],
        in_specs=[pl.BlockSpec(memory_space=pl.ANY)],
        out_specs=[pl.BlockSpec(memory_space=pltpu.VMEM)] * 2,
        scratch_shapes=[
            square,
            square,
            square,
            pltpu.SemaphoreType.DMA((3 * waves,)),
            pltpu.SemaphoreType.DMA((2 * len(units),)),
        ],
        cost_estimate=pl.CostEstimate(flops=work(1.5), bytes_accessed=1 << 20, transcendentals=0),
    )(tiles)


def coupling_kernel(side, groups, tiles, *refs):
    targets, sems = refs[:-1], refs[-1]
    right, top = role()
    inner, outer = (3 - top, 1 - right), (right, 2 + top)
    copies = []
    for units, target in zip(groups, targets):
        copies += load_units(tiles, side, inner, outer, units, target, 0, sems, len(copies))
    for copy in copies:
        copy.wait()


def couplings(tiles, groups):
    side = tiles.shape[1] // 4
    count = sum(len(units) for units in groups)
    return pl.pallas_call(
        functools.partial(coupling_kernel, side, groups),
        name="couplings",
        out_shape=[jax.ShapeDtypeStruct((len(units) * 2 * side, side), jnp.float32) for units in groups],
        in_specs=[pl.BlockSpec(memory_space=pl.ANY)],
        out_specs=[pl.BlockSpec(memory_space=pltpu.VMEM)] * len(groups),
        scratch_shapes=[pltpu.SemaphoreType.DMA((2 * count,))],
        cost_estimate=pl.CostEstimate(flops=work(2), bytes_accessed=2 << 20, transcendentals=0),
    )(tiles)


def parts_of(pack, side, w):
    base = w * height(side)
    return pack[base : base + side, :], pack[base + side : base + 2 * side, :], pack[base + 2 * side : base + 2 * side + 1, :]


def load_blocks(tiles, side, row_sides, col_sides, target, sems):
    copies = []
    for w in range(target.shape[0]):
        for i in range(2):
            for j in range(2):
                place = target.at[w, pl.ds(i * side, side), pl.ds(j * side, side)]
                source = block_of(tiles, side, w, row_sides[i], col_sides[j])
                copies.append(pltpu.make_async_copy(source, place, sems.at[len(copies)]))
                copies[-1].start()
    return copies


def first_kernel(side, own, mate, tiles, solved, rest, coupling, sems):
    waves = solved.shape[0]
    right, top = role()
    loads = load_blocks(tiles, side, (3 - top, 1 - right), (right, 2 + top), coupling, sems)
    ours = [parts_of(own, side, w) for w in range(waves)]
    theirs = [parts_of(mate, side, w) for w in range(waves)]
    inverse = inverses([pack_yy(ours[w][0] + theirs[w][0]) for w in range(waves)])
    for load in loads:
        load.wait()
    for w in range(waves):
        across = jnp.concatenate([ours[w][1], theirs[w][1]], 1)
        gains = mul(inverse[w], jnp.concatenate([across, coupling[w, 0:side, :]], 1))
        solved[w] = gains
        change = mul_t(across, gains)
        rest[w, 0:side, 0:side] = pack_xx(ours[w][0], ours[w][2]) - change[0:side, 0:side]
        rest[w, 0:side, side : 2 * side] = -change[0:side, side : 2 * side]
        rest[w, 0:side, 2 * side :] = coupling[w, side:, :] - change[0:side, 2 * side :]
        rest[w, side:, 0:side] = -change[side:, 0:side]
        rest[w, side:, side : 2 * side] = pack_xx(theirs[w][0], theirs[w][2]) - change[side:, side : 2 * side]
        rest[w, side:, 2 * side :] = -change[side:, 2 * side :]


def second_kernel(side, pack, solved_y, rest, solved, left):
    waves = solved.shape[0]
    parts = [parts_of(pack, side, w) for w in range(waves)]
    inverse = inverses([rest[w, 0:side, 0:side] + pack_xx(parts[w][0], parts[w][2]) for w in range(waves)])
    for w in range(waves):
        vx = parts[w][1]
        gains = mul(inverse[w], jnp.concatenate([vx.T, rest[w, 0:side, side:]], 1))
        solved[w] = gains
        column = jnp.concatenate([vx, rest[w, side:, 0:side], solved_y[w, :, 0:side]], 0)
        change = mul(column, gains)
        left[w, 0:side, 0:side] = pack_yy(parts[w][0]) - change[0:side, 0:side]
        left[w, 0:side, side:] = -change[0:side, side:]
        left[w, side:, 0:side] = -change[side:, 0:side]
        left[w, side : 2 * side, side:] = rest[w, side:, side:] - change[side : 2 * side, side:]
        left[w, 2 * side :, side:] = solved_y[w, :, side:] - change[2 * side :, side:]


def third_kernel(side, pack, solved_x, left, solved, last):
    waves = solved.shape[0]
    parts = [parts_of(pack, side, w) for w in range(waves)]
    inverse = inverses([left[w, 0:side, 0:side] + pack_yy(parts[w][0]) for w in range(waves)])
    for w in range(waves):
        vu = parts[w][1]
        row = jnp.concatenate([left[w, 0:side, side : 2 * side] + vu, left[w, 0:side, 2 * side :]], 1)
        gains = mul(inverse[w], row)
        solved[w] = gains
        column = jnp.concatenate(
            [left[w, side : 2 * side, 0:side] + vu.T, left[w, 2 * side :, 0:side], solved_x[w, :, 0:side]], 0
        )
        change = mul(column, gains)
        uu = pack_xx(parts[w][0], parts[w][2])
        last[w, 0:side, 0:side] = left[w, side : 2 * side, side : 2 * side] + uu - change[0:side, 0:side]
        last[w, 0:side, side:] = left[w, side : 2 * side, 2 * side :] - change[0:side, side:]
        last[w, side : 2 * side, :] = left[w, 2 * side :, side:] - change[side : 2 * side, :]
        last[w, 2 * side :, :] = solved_x[w, :, side:] - change[2 * side :, :]


def fourth_kernel(side, solved_v, last, held):
    waves = last.shape[0]
    inverse = inverses([last[w, 0:side, 0:side] for w in range(waves)])
    for w in range(waves):
        held_u = mul(inverse[w], last[w, 0:side, side:])
        change = mul(jnp.concatenate([last[w, side:, 0:side], solved_v[w, :, 0:side]], 0), held_u)
        held[w, 0] = last[w, side : 2 * side, side:] - change[0:side]
        held[w, 1] = last[w, 2 * side :, side:] - change[side : 2 * side]
        held[w, 2] = solved_v[w, :, side:] - change[2 * side :]
        held[w, 3] = held_u


def whole_call(kernel, name, shapes, time, tiles=None, scratch=()):
    vmem = pl.BlockSpec(memory_space=pltpu.VMEM)

    def call(*args):
        specs = [vmem] * len(args)
        if tiles is not None:
            args = (*args, tiles)
            specs.append(pl.BlockSpec(memory_space=pl.ANY))
        return pl.pallas_call(
            kernel,
            name=name,
            out_shape=[jax.ShapeDtypeStruct(s, jnp.float32) for s in shapes],
            in_specs=specs,
            out_specs=[vmem] * len(shapes),
            scratch_shapes=list(scratch),
            compiler_params=pltpu.CompilerParams(vmem_limit_bytes=32 << 20),
            cost_estimate=pl.CostEstimate(flops=work(time), bytes_accessed=1 << 20, transcendentals=0),
        )(*args)

    return call


def split(x):
    high = x.astype(jnp.bfloat16)
    return high, (x - high.astype(jnp.float32)).astype(jnp.bfloat16)


def mul_split(a, b):
    dims = (((0,), (0,)), ((), ()))
    terms = [(a[0], b[0]), (a[0], b[1]), (a[1], b[0])]
    return sum(lax.dot_general(x, y, dims, preferred_element_type=jnp.float32) for x, y in terms)


MATE, CROSS, FAR = (0, 3), (2, 1), (2, 3)


def columns_kernel(side, groups, with_own, *refs):
    count = len(groups)
    if with_own:
        tiles, held, *arrays = refs[: 2 + count]
        out, coupling, diagonal, load_sems, buffer, sems = refs[2 + count :]
    else:
        _, held, *arrays = refs[: 2 + count]
        out, buffer, sems = refs[2 + count :]
    right, top = role()
    slots = {MATE: 2 * right + 1 - top, CROSS: 2 * (1 - right) + top, FAR: 2 * (1 - right) + 1 - top}
    waves = held.shape[0]
    inner, outer = (3 - top, 1 - right), (right, 2 + top)
    if with_own:
        loads = load_blocks(tiles, side, inner, outer, coupling, load_sems.at[0])
        loads += load_blocks(tiles, side, outer, outer, diagonal, load_sems.at[1])
    parts = {}

    def part(w, i):
        if (w, i) not in parts:
            parts[w, i] = split(held[w, i])
        return parts[w, i]

    def product(w, box, block):
        total = 0.0
        for n, i in enumerate(box):
            total += mul_split(part(w, i), split(block[n * side : (n + 1) * side]))
        return total

    stores = []

    def put(w, slot, j, value):
        n = len(stores)
        width = value.shape[1]
        buffer[n, :, 0:width] = value
        column = pl.multiple_of(slot * 2 * side + j * side, side)
        target = out.at[w, :, pl.ds(column, width)]
        stores.append(pltpu.make_async_copy(buffer.at[n, :, pl.ds(0, width)], target, sems.at[n]))
        stores[-1].start()

    for (box, units, base), array in zip(groups, arrays):
        n = 0
        while n < len(units):
            w, j = divmod(units[n], 2)
            pair = j == 0 and n + 1 < len(units) and units[n + 1] == units[n] + 1
            rows = [array[base + 2 * side * m : base + 2 * side * (m + 1), :] for m in range(n, n + 1 + pair)]
            block = jnp.concatenate(rows, 1)
            put(w, slots[box], j, -product(w, box, block))
            n += 2 if pair else 1
    if with_own:
        for load in loads:
            load.wait()
        for w in range(waves):
            put(w, 2 * right + top, 0, diagonal[w] - product(w, (0, 1), coupling[w]))
    for store in stores:
        store.wait()


def columns_call(name, time, source, held, pieces, with_own):
    waves, side = held.shape[0], held.shape[2]
    groups = tuple((box, units, base) for box, units, _, base in pieces)
    vmem, anywhere = pl.BlockSpec(memory_space=pltpu.VMEM), pl.BlockSpec(memory_space=pl.ANY)
    square = pltpu.VMEM((waves, 2 * side, 2 * side), jnp.float32)
    most = sum(len(units) for _, units, _, _ in pieces) + waves
    scratch = [pltpu.VMEM((most, 2 * side, 2 * side), jnp.float32), pltpu.SemaphoreType.DMA((most,))]
    if with_own:
        scratch = [square, square, pltpu.SemaphoreType.DMA((2, 4 * waves))] + scratch
    return pl.pallas_call(
        functools.partial(columns_kernel, side, groups, with_own),
        name=name,
        out_shape=jax.ShapeDtypeStruct((waves, 2 * side, 8 * side), jnp.float32),
        in_specs=[anywhere] + [vmem] * (1 + len(pieces)),
        out_specs=anywhere,
        scratch_shapes=scratch,
        input_output_aliases={} if with_own else {0: 0},
        compiler_params=pltpu.CompilerParams(vmem_limit_bytes=32 << 20),
        cost_estimate=pl.CostEstimate(flops=work(time), bytes_accessed=1 << 20, transcendentals=0),
    )(source, held, *(array for _, _, array, _ in pieces))


def body(children):
    tiles = children[:, 0, 0]
    waves, side = tiles.shape[0], tiles.shape[1] // 4
    units = tuple(range(2 * waves))
    first, second = units[:1], units[1:]
    base = waves * height(side)
    own, sent = packed(tiles, first)
    whole, part = couplings(tiles, (units, second))
    cross_0 = swapped(sent, "gx")
    mate_pack = swapped(own, "gy")
    mate = swapped(after(whole, mate_pack), "gy")

    def eliminate(kernel, name, shapes, time, **more):
        shapes = [(waves, *shape) for shape in shapes]
        return whole_call(functools.partial(kernel, side), name, shapes, time, **more)

    full = 4 * side
    loads = [pltpu.VMEM((waves, 2 * side, 2 * side), jnp.float32), pltpu.SemaphoreType.DMA((4 * waves,))]
    solved_y, rest = eliminate(
        first_kernel, "eliminate_y", [(side, full), (2 * side, full)], 1, tiles=tiles, scratch=loads
    )(own, mate_pack)
    cross_1 = swapped(after(part, (cross_0, solved_y)), "gx")
    far_0 = swapped(cross_0, "gy")
    solved_x, left = eliminate(second_kernel, "eliminate_x", [(side, full), (3 * side, full)], 6)(
        cross_0, solved_y, rest
    )
    solved_v, last = eliminate(third_kernel, "eliminate_v", [(side, 3 * side), (3 * side, 3 * side)], 6)(
        far_0, solved_x, left
    )
    far_1 = swapped(after(cross_1, solved_v), "gy")
    (held,) = eliminate(fourth_kernel, "eliminate_u", [(4, side, 2 * side)], 5)(solved_v, last)
    near = columns_call(
        "near_columns",
        3,
        tiles,
        held,
        [(MATE, units, mate, 0), (CROSS, first, cross_0, base), (FAR, first, far_0, base), (CROSS, second, cross_1, 0)],
        True,
    )
    merged = columns_call("last_columns", 1.5, near, held, [(FAR, second, far_1, 0)], False)
    return merged[:, None, None]


def solution(mesh):
    placed = (P("groups", "gx", "gy", None, None),)
    return jax.shard_map(
        body,
        mesh=mesh,
        in_specs=placed,
        out_specs=P("groups", "gx", "gy", None, None),
        check_vma=False,
    )
```

time: 60.6 us -> 55 us (0.908)
  waiting for transfers between devices: 1.97 us -> 12.4 us
  starting transfers between devices: 18.4 us -> 9.87 us
  Pallas kernels: 38.7 us -> 32.2 us
  local copies, waits for them, and re-layouts: 1.06 us -> 0.01 us
    ppermute x10 -> x6, waiting for transfers between devices: 1.97 us -> 12.4 us  [swapped(): return lax.ppermute(block, axis, route)]
    ppermute x10 -> x6, starting transfers between devices: 18.4 us -> 9.87 us  [swapped(): return lax.ppermute(block, axis, route)]
    pallas_call x8, Pallas kernels: 38.7 us -> 32.2 us  [the longest x4 23.8 us: call(): pl.pallas_call(kernel, name=name, out_shape=[jax.ShapeDtypeStruct(s, jnp....]
    unnamed x14 -> x6, local copies, waits for them, and re-layouts: 1.06 us -> 0.01 us
  transfers between devices with their start and end apart: 10 -> 6, of which waited for: 3 -> 4; matrix products, arithmetic and copies ran while one was open for 0% -> 0% of each run, Pallas kernels for 58% -> 53%
where the time goes in v3:
time: 55 us; the launch traced here: 54.8 us
  Pallas kernels  32.2 us (59%)
  waiting for transfers between devices  12.4 us (23%)
  starting transfers between devices  9.87 us (18%)
    pallas_call x4, Pallas kernels, call(): pl.pallas_call(kernel, name=name, out_shape=[jax.ShapeDtypeStruct(s, jnp....  23.8 us
    ppermute x6, waiting for transfers between devices, swapped(): return lax.ppermute(block, axis, route)  12.4 us
    ppermute x6, starting transfers between devices, swapped(): return lax.ppermute(block, axis, route)  9.87 us
    pallas_call x2, Pallas kernels, columns_call(): pl.pallas_call(functools.partial(columns_kernel, side, groups, with_own),...  4.21 us
    pallas_call x1, Pallas kernels, couplings(): pl.pallas_call(functools.partial(coupling_kernel, side, groups), name='co...  2.26 us
    pallas_call x1, Pallas kernels, packed(): pl.pallas_call(functools.partial(pack_kernel, side, units), name='pack',...  2 us
  transfers between devices with their start and end apart: 6, of which 4 were waited for; matrix products, arithmetic and copies ran while one was open for 0% of the time, Pallas kernels for 53%

profile of v3, /device:TPU:0, one launch (start us, length us, event | category | flops | bytes accessed | tf_op | source)
XLA Modules:
  0.0 54.8 jit_solution(1640118291645809041)
XLA Ops:
  0.0 2.0 %pack.1 = (f32[528,128]{1,0:T(8,128)}, f32[784,128]{1,0:T(8,128)}) custom-call(f32[2,512,512]{2,1,0:T(8,128)} %bitcast.4), custom_call_target="tpu_custom_call" | custom-call | flops 1500000000 | bytes 1048576 | tf_op jit(solution)/shard_map/pack/pallas_call | solution.py:179
  2.0 4.1 %collective-permute-start = (f32[784,128]{1,0:T(8,128)}, f32[784,128]{1,0:T(8,128)S(1)}, u32[]{:S(2)}, u32[]{:S(2)}) collective-permute-start(f32[784,128]{1,0:T(8,128)} %get-tuple-element.18), channel_id=1, source_target_pairs={{0,8},{8,0},{4,12},{12,4},{1,9},{9,1},{5,13},{13,5},{2,10},{10,2},... | collective-permute-start | bytes 1204232 | tf_op jit(solution)/shard_map/ppermute | solution.py:21
  6.1 0.0 copy-start
  6.1 0.0 copy-start.1
  6.1 1.5 %collective-permute-start.2 = (f32[528,128]{1,0:T(8,128)}, f32[528,128]{1,0:T(8,128)S(1)}, u32[]{:S(2)}, u32[]{:S(2)}) collective-permute-start(f32[528,128]{1,0:T(8,128)} %get-tuple-element.19.own), channel_id=1, source_target_pairs={{0,2},{2,0},{1,3},{3,1},{4,6},{6,4},{5,7},{7,5},{8,10},{10,8},{9,1... | collective-permute-start | bytes 811016 | tf_op jit(solution)/shard_map/ppermute | solution.py:21
  7.6 2.3 %couplings.1 = (f32[1024,128]{1,0:T(8,128)}, f32[768,128]{1,0:T(8,128)}) custom-call(f32[2,512,512]{2,1,0:T(8,128)} %bitcast.5), custom_call_target="tpu_custom_call" | custom-call | flops 2000000000 | bytes 2097152 | tf_op jit(solution)/shard_map/couplings/pallas_call | solution.py:213
  9.9 0.0 copy-start.2
  9.9 4.4 %collective-permute-done.2.mate = f32[528,128]{1,0:T(8,128)S(1)} collective-permute-done((f32[528,128]{1,0:T(8,128)}, f32[528,128]{1,0:T(8,128)S(1)}, u32[]{:S(2)}, u32[]{:S(2)}) %collective-permute-start.2) | collective-permute-done | bytes 270368 | tf_op jit(solution)/shard_map/ppermute | solution.py:21
  14.3 1.5 %collective-permute-start.3 = (f32[1024,128]{1,0:T(8,128)}, f32[1024,128]{1,0:T(8,128)S(1)}, u32[]{:S(2)}, u32[]{:S(2)}) collective-permute-start(f32[1024,128]{1,0:T(8,128)} %get-tuple-element.27), channel_id=1, source_target_pairs={{0,2},{2,0},{1,3},{3,1},{4,6},{6,4},{5,7},{7,5},{8,10},{10,8},{9,1... | collective-permute-start | bytes 1572872 | tf_op jit(solution)/shard_map/ppermute | solution.py:21
  15.8 0.0 copy-done
  15.8 0.0 copy-done.1
  15.8 6.1 %eliminate_y.1 = (f32[2,128,512]{2,1,0:T(8,128)S(1)}, f32[2,256,512]{2,1,0:T(8,128)S(1)}) custom-call(f32[528,128]{1,0:T(8,128)S(1)} %copy-done.1, f32[528,128]{1,0:T(8,128)S(1)} %collective-permute-done.2.mate, f32[2,512,512]{2,1,0:T(8,128)S(1)} %bitcast.6), custom_call_target="tpu_custom_call" | custom-call | flops 1000000000 | bytes 1048576 | tf_op jit(solution)/shard_map/eliminate_y/pallas_call | solution.py:320
  21.8 2.4 %collective-permute-done.pack.refs_3_ = f32[784,128]{1,0:T(8,128)S(1)} collective-permute-done((f32[784,128]{1,0:T(8,128)}, f32[784,128]{1,0:T(8,128)S(1)}, u32[]{:S(2)}, u32[]{:S(2)}) %collective-permute-start) | collective-permute-done | bytes 401440 | tf_op jit(solution)/shard_map/ppermute | solution.py:21
  24.2 0.0 copy-done.2
  24.2 0.0 collective-permute-start.4
  24.2 1.5 %collective-permute-start.1 = (f32[784,128]{1,0:T(8,128)S(1)}, f32[784,128]{1,0:T(8,128)S(1)}, u32[]{:S(2)}, u32[]{:S(2)}) collective-permute-start(f32[784,128]{1,0:T(8,128)S(1)} %collective-permute-done.pack.refs_3_), channel_id=1, source_target_pairs={{0,2},{2,0},{1,3},{3,1},{4,6},{6,4},{5,7},{7,5},{8,10},{10,8},{9,1... | collective-permute-start | bytes 1204232 | tf_op jit(solution)/shard_map/ppermute | solution.py:21
  25.8 6.3 %eliminate_x.1 = (f32[2,128,512]{2,1,0:T(8,128)S(1)}, f32[2,384,512]{2,1,0:T(8,128)S(1)}) custom-call(f32[784,128]{1,0:T(8,128)S(1)} %collective-permute-done.pack.refs_3_, f32[2,128,512]{2,1,0:T(8,128)S(1)} %get-tuple-element.20.solved_y, f32[2,256,512]{2,1,0:T(8,128)S(1)} %get-tuple-element.21.rest), custom_call_target="tpu_custom_call" | custom-call | flops 6000000000 | bytes 1048576 | tf_op jit(solution)/shard_map/eliminate_x/pallas_call | solution.py:320
  32.1 3.5 %collective-permute-done.1.pack.refs_4_ = f32[784,128]{1,0:T(8,128)S(1)} collective-permute-done((f32[784,128]{1,0:T(8,128)S(1)}, f32[784,128]{1,0:T(8,128)S(1)}, u32[]{:S(2)}, u32[]{:S(2)}) %collective-permute-start.1) | collective-permute-done | bytes 401440 | tf_op jit(solution)/shard_map/ppermute | solution.py:21
  35.6 6.1 %eliminate_v.1 = (f32[2,128,384]{2,1,0:T(8,128)S(1)}, f32[2,384,384]{2,1,0:T(8,128)S(1)}) custom-call(f32[784,128]{1,0:T(8,128)S(1)} %collective-permute-done.1.pack.refs_4_, f32[2,128,512]{2,1,0:T(8,128)S(1)} %get-tuple-element.22.solved_x, f32[2,384,512]{2,1,0:T(8,128)S(1)} %get-tuple-element.23.left), custom_call_target="tpu_custom_call" | custom-call | flops 6000000000 | bytes 1048576 | tf_op jit(solution)/shard_map/eliminate_v/pallas_call | solution.py:320
  41.7 2.2 %collective-permute-done.4.refs_5_ = f32[768,128]{1,0:T(8,128)S(1)} collective-permute-done((f32[768,128]{1,0:T(8,128)S(1)}, f32[768,128]{1,0:T(8,128)S(1)}, u32[]{:S(2)}, u32[]{:S(2)}) %collective-permute-start.4) | collective-permute-done | bytes 393248 | tf_op jit(solution)/shard_map/ppermute | solution.py:21
  43.8 1.2 %collective-permute-start.5 = (f32[768,128]{1,0:T(8,128)S(1)}, f32[768,128]{1,0:T(8,128)S(1)}, u32[]{:S(2)}, u32[]{:S(2)}) collective-permute-start(f32[768,128]{1,0:T(8,128)S(1)} %collective-permute-done.4.refs_5_), channel_id=1, source_target_pairs={{0,2},{2,0},{1,3},{3,1},{4,6},{6,4},{5,7},{7,5},{8,10},{10,8},{9,1... | collective-permute-start | bytes 1179656 | tf_op jit(solution)/shard_map/ppermute | solution.py:21
  45.1 5.3 %eliminate_u.1.refs_1_ = f32[2,4,128,256]{3,2,1,0:T(8,128)S(1)} custom-call(f32[2,128,384]{2,1,0:T(8,128)S(1)} %get-tuple-element.24.solved_v, f32[2,384,384]{2,1,0:T(8,128)S(1)} %get-tuple-element.25.last), custom_call_target="tpu_custom_call" | custom-call | flops 5000000000 | bytes 1048576 | tf_op jit(solution)/shard_map/eliminate_u/pallas_call | solution.py:320
  50.4 0.0 collective-permute-done.3.refs_2_
  50.4 3.0 %near_columns.1.refs_0_ = f32[2,256,1024]{2,1,0:T(8,128)} custom-call(f32[2,512,512]{2,1,0:T(8,128)S(1)} %bitcast.7, f32[2,4,128,256]{3,2,1,0:T(8,128)S(1)} %eliminate_u.1.refs_1_, f32[1024,128]{1,0:T(8,128)S(1)} %collective-permute-done.3.refs_2_, f32[784,128]{1,0:T(8,128)S(1)} %collective-permute-done.pack.refs_3_, ...), custom_call_target="tpu_custom_call" | custom-call | flops 3000000000 | bytes 1048576 | tf_op jit(solution)/shard_map/near_columns/pallas_call | solution.py:414
  53.4 0.0 collective-permute-done.5.refs_2_
  53.4 1.3 %last_columns.1 = f32[2,256,1024]{2,1,0:T(8,128)} custom-call(f32[2,256,1024]{2,1,0:T(8,128)} %near_columns.1.refs_0_, f32[2,4,128,256]{3,2,1,0:T(8,128)S(1)} %eliminate_u.1.refs_1_, f32[768,128]{1,0:T(8,128)S(1)} %collective-permute-done.5.refs_2_), custom_call_target="tpu_custom_call", output_to_operand_aliasing={{}: (0, {})} | custom-call | flops 1500000000 | bytes 1048576 | tf_op jit(solution)/shard_map/last_columns/pallas_call | solution.py:414
Async XLA Ops:
  2.0 22.2 %collective-permute-start = (f32[784,128]{1,0:T(8,128)}, f32[784,128]{1,0:T(8,128)S(1)}, u32[]{:S(2)}, u32[]{:S(2)}) collective-permute-start(f32[784,128]{1,0:T(8,128)} %get-tuple-element.18), channel_id=1, source_target_pairs={{0,8},{8,0},{4,12},{12,4},{1,9},{9,1},{5,13},{13,5},{2,10},{10,2},... | collective-permute-start | bytes 1204232 | tf_op jit(solution)/shard_map/ppermute | solution.py:21
  6.1 9.7 %copy-start = (f32[2,1,1,512,512]{4,3,2,1,0:T(8,128)S(1)}, f32[2,1,1,512,512]{4,3,2,1,0:T(8,128)}, u32[]{:S(2)}) copy-start(f32[2,1,1,512,512]{4,3,2,1,0:T(8,128)} %param.1) | copy-start | bytes 6291460
  6.1 9.7 %copy-start.1 = (f32[528,128]{1,0:T(8,128)S(1)}, f32[528,128]{1,0:T(8,128)}, u32[]{:S(2)}) copy-start(f32[528,128]{1,0:T(8,128)} %get-tuple-element.19.own) | copy-start | bytes 811012
  6.1 8.2 %collective-permute-start.2 = (f32[528,128]{1,0:T(8,128)}, f32[528,128]{1,0:T(8,128)S(1)}, u32[]{:S(2)}, u32[]{:S(2)}) collective-permute-start(f32[528,128]{1,0:T(8,128)} %get-tuple-element.19.own), channel_id=1, source_target_pairs={{0,2},{2,0},{1,3},{3,1},{4,6},{6,4},{5,7},{7,5},{8,10},{10,8},{9,1... | collective-permute-start | bytes 811016 | tf_op jit(solution)/shard_map/ppermute | solution.py:21
  9.9 14.3 %copy-start.2 = (f32[768,128]{1,0:T(8,128)S(1)}, f32[768,128]{1,0:T(8,128)}, u32[]{:S(2)}) copy-start(f32[768,128]{1,0:T(8,128)} %get-tuple-element.29) | copy-start | bytes 1179652
  14.3 36.1 %collective-permute-start.3 = (f32[1024,128]{1,0:T(8,128)}, f32[1024,128]{1,0:T(8,128)S(1)}, u32[]{:S(2)}, u32[]{:S(2)}) collective-permute-start(f32[1024,128]{1,0:T(8,128)} %get-tuple-element.27), channel_id=1, source_target_pairs={{0,2},{2,0},{1,3},{3,1},{4,6},{6,4},{5,7},{7,5},{8,10},{10,8},{9,1... | collective-permute-start | bytes 1572872 | tf_op jit(solution)/shard_map/ppermute | solution.py:21
  24.2 19.6 %collective-permute-start.4 = (f32[768,128]{1,0:T(8,128)S(1)}, f32[768,128]{1,0:T(8,128)S(1)}, u32[]{:S(2)}, u32[]{:S(2)}) collective-permute-start(f32[768,128]{1,0:T(8,128)S(1)} %copy-done.2), channel_id=1, source_target_pairs={{0,8},{8,0},{4,12},{12,4},{1,9},{9,1},{5,13},{13,5},{2,10},{10,2},... | collective-permute-start | bytes 1179656 | tf_op jit(solution)/shard_map/ppermute | solution.py:21
  24.2 11.3 %collective-permute-start.1 = (f32[784,128]{1,0:T(8,128)S(1)}, f32[784,128]{1,0:T(8,128)S(1)}, u32[]{:S(2)}, u32[]{:S(2)}) collective-permute-start(f32[784,128]{1,0:T(8,128)S(1)} %collective-permute-done.pack.refs_3_), channel_id=1, source_target_pairs={{0,2},{2,0},{1,3},{3,1},{4,6},{6,4},{5,7},{7,5},{8,10},{10,8},{9,1... | collective-permute-start | bytes 1204232 | tf_op jit(solution)/shard_map/ppermute | solution.py:21
  43.8 9.5 %collective-permute-start.5 = (f32[768,128]{1,0:T(8,128)S(1)}, f32[768,128]{1,0:T(8,128)S(1)}, u32[]{:S(2)}, u32[]{:S(2)}) collective-permute-start(f32[768,128]{1,0:T(8,128)S(1)} %collective-permute-done.4.refs_5_), channel_id=1, source_target_pairs={{0,2},{2,0},{1,3},{3,1},{4,6},{6,4},{5,7},{7,5},{8,10},{10,8},{9,1... | collective-permute-start | bytes 1179656 | tf_op jit(solution)/shard_map/ppermute | solution.py:21

commit v4 on v3

--- a/solution.py
+++ b/solution.py
@@ -266,15 +266,24 @@
     inverse = inverses([rest[w, 0:side, 0:side] + pack_xx(parts[w][0], parts[w][2]) for w in range(waves)])
     for w in range(waves):
         vx = parts[w][1]
-        gains = mul(inverse[w], jnp.concatenate([vx.T, rest[w, 0:side, side:]], 1))
-        solved[w] = gains
-        column = jnp.concatenate([vx, rest[w, side:, 0:side], solved_y[w, :, 0:side]], 0)
+        gains = mul(inverse[w], jnp.concatenate([vx.T, rest[w, 0:side, side : 2 * side]], 1))
+        right_gains = mul_split(split(inverse[w]), split(rest[w, 0:side, 2 * side :]), 1)
+        solved[w, :, 0 : 2 * side] = gains
+        solved[w, :, 2 * side :] = right_gains
+        column = jnp.concatenate([vx, rest[w, side:, 0:side]], 0)
+        column_y = solved_y[w, :, 0:side]
         change = mul(column, gains)
+        change_y = mul_split(split(column_y), split(gains), 1)
+        right_change = mul_split(split(jnp.concatenate([column, column_y], 0)), split(right_gains), 1)
         left[w, 0:side, 0:side] = pack_yy(parts[w][0]) - change[0:side, 0:side]
-        left[w, 0:side, side:] = -change[0:side, side:]
-        left[w, side:, 0:side] = -change[side:, 0:side]
-        left[w, side : 2 * side, side:] = rest[w, side:, side:] - change[side : 2 * side, side:]
-        left[w, 2 * side :, side:] = solved_y[w, :, side:] - change[2 * side :, side:]
+        left[w, 0:side, side : 2 * side] = -change[0:side, side:]
+        left[w, 0:side, 2 * side :] = -right_change[0:side]
+        left[w, side : 2 * side, 0:side] = -change[side:, 0:side]
+        left[w, side : 2 * side, side : 2 * side] = rest[w, side:, side : 2 * side] - change[side:, side:]
+        left[w, side : 2 * side, 2 * side :] = rest[w, side:, 2 * side :] - right_change[side : 2 * side]
+        left[w, 2 * side :, 0:side] = -change_y[:, 0:side]
+        left[w, 2 * side :, side : 2 * side] = solved_y[w, :, side : 2 * side] - change_y[:, side:]
+        left[w, 2 * side :, 2 * side :] = solved_y[w, :, 2 * side :] - right_change[2 * side :]
 
 
 def third_kernel(side, pack, solved_x, left, solved, last):
@@ -283,26 +292,30 @@
     inverse = inverses([left[w, 0:side, 0:side] + pack_yy(parts[w][0]) for w in range(waves)])
     for w in range(waves):
         vu = parts[w][1]
-        row = jnp.concatenate([left[w, 0:side, side : 2 * side] + vu, left[w, 0:side, 2 * side :]], 1)
-        gains = mul(inverse[w], row)
-        solved[w] = gains
-        column = jnp.concatenate(
-            [left[w, side : 2 * side, 0:side] + vu.T, left[w, 2 * side :, 0:side], solved_x[w, :, 0:side]], 0
-        )
-        change = mul(column, gains)
+        gains = mul(inverse[w], left[w, 0:side, side : 2 * side] + vu)
+        right_gains = mul_split(split(inverse[w]), split(left[w, 0:side, 2 * side :]), 1)
+        solved[w, :, 0:side] = gains
+        solved[w, :, side:] = right_gains
+        column_u = left[w, side : 2 * side, 0:side] + vu.T
+        column_yx = jnp.concatenate([left[w, 2 * side :, 0:side], solved_x[w, :, 0:side]], 0)
         uu = pack_xx(parts[w][0], parts[w][2])
-        last[w, 0:side, 0:side] = left[w, side : 2 * side, side : 2 * side] + uu - change[0:side, 0:side]
-        last[w, 0:side, side:] = left[w, side : 2 * side, 2 * side :] - change[0:side, side:]
-        last[w, side : 2 * side, :] = left[w, 2 * side :, side:] - change[side : 2 * side, :]
-        last[w, 2 * side :, :] = solved_x[w, :, side:] - change[2 * side :, :]
+        last[w, 0:side, 0:side] = left[w, side : 2 * side, side : 2 * side] + uu - mul(column_u, gains)
+        change = mul_split(split(column_yx), split(gains), 1)
+        right_change = mul_split(split(jnp.concatenate([column_u, column_yx], 0)), split(right_gains), 1)
+        last[w, 0:side, side:] = left[w, side : 2 * side, 2 * side :] - right_change[0:side]
+        last[w, side : 2 * side, 0:side] = left[w, 2 * side :, side : 2 * side] - change[0:side]
+        last[w, side : 2 * side, side:] = left[w, 2 * side :, 2 * side :] - right_change[side : 2 * side]
+        last[w, 2 * side :, 0:side] = solved_x[w, :, side : 2 * side] - change[side:]
+        last[w, 2 * side :, side:] = solved_x[w, :, 2 * side :] - right_change[2 * side :]
 
 
 def fourth_kernel(side, solved_v, last, held):
     waves = last.shape[0]
     inverse = inverses([last[w, 0:side, 0:side] for w in range(waves)])
     for w in range(waves):
-        held_u = mul(inverse[w], last[w, 0:side, side:])
-        change = mul(jnp.concatenate([last[w, side:, 0:side], solved_v[w, :, 0:side]], 0), held_u)
+        held_u = mul_split(split(inverse[w]), split(last[w, 0:side, side:]), 1)
+        column = jnp.concatenate([last[w, side:, 0:side], solved_v[w, :, 0:side]], 0)
+        change = mul_split(split(column), split(held_u), 1)
         held[w, 0] = last[w, side : 2 * side, side:] - change[0:side]
         held[w, 1] = last[w, 2 * side :, side:] - change[side : 2 * side]
         held[w, 2] = solved_v[w, :, side:] - change[2 * side :]
@@ -336,8 +349,8 @@
     return high, (x - high.astype(jnp.float32)).astype(jnp.bfloat16)
 
 
-def mul_split(a, b):
-    dims = (((0,), (0,)), ((), ()))
+def mul_split(a, b, along=0):
+    dims = (((along,), (0,)), ((), ()))
     terms = [(a[0], b[0]), (a[0], b[1]), (a[1], b[0])]
     return sum(lax.dot_general(x, y, dims, preferred_element_type=jnp.float32) for x, y in terms)
 
@@ -362,16 +375,10 @@
         loads += load_blocks(tiles, side, outer, outer, diagonal, load_sems.at[1])
     parts = {}
 
-    def part(w, i):
-        if (w, i) not in parts:
-            parts[w, i] = split(held[w, i])
-        return parts[w, i]
-
     def product(w, box, block):
-        total = 0.0
-        for n, i in enumerate(box):
-            total += mul_split(part(w, i), split(block[n * side : (n + 1) * side]))
-        return total
+        if (w, box) not in parts:
+            parts[w, box] = split(jnp.concatenate([held[w, i] for i in box], 0))
+        return mul_split(parts[w, box], split(block))
 
     stores = []
 

time: 55 us -> 54.8 us (level)
  Pallas kernels: 32.2 us -> 29.8 us
  waiting for transfers between devices: 12.4 us -> 14.6 us
    ppermute x6, waiting for transfers between devices: 12.4 us -> 14.6 us  [swapped(): return lax.ppermute(block, axis, route)]
    pallas_call x4, Pallas kernels: 23.8 us -> 21.9 us  [call(): pl.pallas_call(kernel, name=name, out_shape=[jax.ShapeDtypeStruct(s, jnp....]
    pallas_call x2, Pallas kernels: 4.21 us -> 3.62 us  [columns_call(): pl.pallas_call(functools.partial(columns_kernel, side, groups, with_own),...]
  transfers between devices with their start and end apart: 6 -> 6, of which waited for: 4 -> 5; matrix products, arithmetic and copies ran while one was open for 0% -> 0% of each run, Pallas kernels for 53% -> 49%
where the time goes in v4:
time: 54.8 us; the launch traced here: 54.5 us
  Pallas kernels  29.8 us (54%)
  waiting for transfers between devices  14.6 us (27%)
  starting transfers between devices  9.87 us (18%)
    pallas_call x4, Pallas kernels, call(): pl.pallas_call(kernel, name=name, out_shape=[jax.ShapeDtypeStruct(s, jnp....  21.9 us
    ppermute x6, waiting for transfers between devices, swapped(): return lax.ppermute(block, axis, route)  14.6 us
    ppermute x6, starting transfers between devices, swapped(): return lax.ppermute(block, axis, route)  9.87 us
    pallas_call x2, Pallas kernels, columns_call(): pl.pallas_call(functools.partial(columns_kernel, side, groups, with_own),...  3.62 us
    pallas_call x1, Pallas kernels, couplings(): pl.pallas_call(functools.partial(coupling_kernel, side, groups), name='co...  2.26 us
    pallas_call x1, Pallas kernels, packed(): pl.pallas_call(functools.partial(pack_kernel, side, units), name='pack',...  2 us
  transfers between devices with their start and end apart: 6, of which 5 were waited for; matrix products, arithmetic and copies ran while one was open for 0% of the time, Pallas kernels for 49%

profile of v4, /device:TPU:0, one launch (start us, length us, event | category | flops | bytes accessed | tf_op | source)
XLA Modules:
  0.0 54.5 jit_solution(4398636004157834900)
XLA Ops:
  0.0 2.0 %pack.1 = (f32[528,128]{1,0:T(8,128)}, f32[784,128]{1,0:T(8,128)}) custom-call(f32[2,512,512]{2,1,0:T(8,128)} %bitcast.4), custom_call_target="tpu_custom_call" | custom-call | flops 1500000000 | bytes 1048576 | tf_op jit(solution)/shard_map/pack/pallas_call | solution.py:179
  2.0 4.1 %collective-permute-start = (f32[784,128]{1,0:T(8,128)}, f32[784,128]{1,0:T(8,128)S(1)}, u32[]{:S(2)}, u32[]{:S(2)}) collective-permute-start(f32[784,128]{1,0:T(8,128)} %get-tuple-element.18), channel_id=1, source_target_pairs={{0,8},{8,0},{4,12},{12,4},{1,9},{9,1},{5,13},{13,5},{2,10},{10,2},... | collective-permute-start | bytes 1204232 | tf_op jit(solution)/shard_map/ppermute | solution.py:21
  6.1 0.0 copy-start
  6.1 0.0 copy-start.1
  6.1 1.5 %collective-permute-start.2 = (f32[528,128]{1,0:T(8,128)}, f32[528,128]{1,0:T(8,128)S(1)}, u32[]{:S(2)}, u32[]{:S(2)}) collective-permute-start(f32[528,128]{1,0:T(8,128)} %get-tuple-element.19.own), channel_id=1, source_target_pairs={{0,2},{2,0},{1,3},{3,1},{4,6},{6,4},{5,7},{7,5},{8,10},{10,8},{9,1... | collective-permute-start | bytes 811016 | tf_op jit(solution)/shard_map/ppermute | solution.py:21
  7.6 2.3 %couplings.1 = (f32[1024,128]{1,0:T(8,128)}, f32[768,128]{1,0:T(8,128)}) custom-call(f32[2,512,512]{2,1,0:T(8,128)} %bitcast.5), custom_call_target="tpu_custom_call" | custom-call | flops 2000000000 | bytes 2097152 | tf_op jit(solution)/shard_map/couplings/pallas_call | solution.py:213
  9.9 0.0 copy-start.2
  9.9 4.4 %collective-permute-done.2.mate = f32[528,128]{1,0:T(8,128)S(1)} collective-permute-done((f32[528,128]{1,0:T(8,128)}, f32[528,128]{1,0:T(8,128)S(1)}, u32[]{:S(2)}, u32[]{:S(2)}) %collective-permute-start.2) | collective-permute-done | bytes 270368 | tf_op jit(solution)/shard_map/ppermute | solution.py:21
  14.3 1.5 %collective-permute-start.3 = (f32[1024,128]{1,0:T(8,128)}, f32[1024,128]{1,0:T(8,128)S(1)}, u32[]{:S(2)}, u32[]{:S(2)}) collective-permute-start(f32[1024,128]{1,0:T(8,128)} %get-tuple-element.27), channel_id=1, source_target_pairs={{0,2},{2,0},{1,3},{3,1},{4,6},{6,4},{5,7},{7,5},{8,10},{10,8},{9,1... | collective-permute-start | bytes 1572872 | tf_op jit(solution)/shard_map/ppermute | solution.py:21
  15.8 0.0 copy-done
  15.8 0.0 copy-done.1
  15.8 6.1 %eliminate_y.1 = (f32[2,128,512]{2,1,0:T(8,128)S(1)}, f32[2,256,512]{2,1,0:T(8,128)S(1)}) custom-call(f32[528,128]{1,0:T(8,128)S(1)} %copy-done.1, f32[528,128]{1,0:T(8,128)S(1)} %collective-permute-done.2.mate, f32[2,512,512]{2,1,0:T(8,128)S(1)} %bitcast.6), custom_call_target="tpu_custom_call" | custom-call | flops 1000000000 | bytes 1048576 | tf_op jit(solution)/shard_map/eliminate_y/pallas_call | solution.py:333
  21.8 2.4 %collective-permute-done.pack.refs_3_ = f32[784,128]{1,0:T(8,128)S(1)} collective-permute-done((f32[784,128]{1,0:T(8,128)}, f32[784,128]{1,0:T(8,128)S(1)}, u32[]{:S(2)}, u32[]{:S(2)}) %collective-permute-start) | collective-permute-done | bytes 401440 | tf_op jit(solution)/shard_map/ppermute | solution.py:21
  24.2 0.0 copy-done.2
  24.2 0.0 collective-permute-start.4
  24.2 1.5 %collective-permute-start.1 = (f32[784,128]{1,0:T(8,128)S(1)}, f32[784,128]{1,0:T(8,128)S(1)}, u32[]{:S(2)}, u32[]{:S(2)}) collective-permute-start(f32[784,128]{1,0:T(8,128)S(1)} %collective-permute-done.pack.refs_3_), channel_id=1, source_target_pairs={{0,2},{2,0},{1,3},{3,1},{4,6},{6,4},{5,7},{7,5},{8,10},{10,8},{9,1... | collective-permute-start | bytes 1204232 | tf_op jit(solution)/shard_map/ppermute | solution.py:21
  25.8 5.8 %eliminate_x.1 = (f32[2,128,512]{2,1,0:T(8,128)S(1)}, f32[2,384,512]{2,1,0:T(8,128)S(1)}) custom-call(f32[784,128]{1,0:T(8,128)S(1)} %collective-permute-done.pack.refs_3_, f32[2,128,512]{2,1,0:T(8,128)S(1)} %get-tuple-element.20.solved_y, f32[2,256,512]{2,1,0:T(8,128)S(1)} %get-tuple-element.21.rest), custom_call_target="tpu_custom_call" | custom-call | flops 6000000000 | bytes 1048576 | tf_op jit(solution)/shard_map/eliminate_x/pallas_call | solution.py:333
  31.5 4.0 %collective-permute-done.1.pack.refs_4_ = f32[784,128]{1,0:T(8,128)S(1)} collective-permute-done((f32[784,128]{1,0:T(8,128)S(1)}, f32[784,128]{1,0:T(8,128)S(1)}, u32[]{:S(2)}, u32[]{:S(2)}) %collective-permute-start.1) | collective-permute-done | bytes 401440 | tf_op jit(solution)/shard_map/ppermute | solution.py:21
  35.6 5.3 %eliminate_v.1 = (f32[2,128,384]{2,1,0:T(8,128)S(1)}, f32[2,384,384]{2,1,0:T(8,128)S(1)}) custom-call(f32[784,128]{1,0:T(8,128)S(1)} %collective-permute-done.1.pack.refs_4_, f32[2,128,512]{2,1,0:T(8,128)S(1)} %get-tuple-element.22.solved_x, f32[2,384,512]{2,1,0:T(8,128)S(1)} %get-tuple-element.23.left), custom_call_target="tpu_custom_call" | custom-call | flops 6000000000 | bytes 1048576 | tf_op jit(solution)/shard_map/eliminate_v/pallas_call | solution.py:333
  40.9 3.0 %collective-permute-done.4.refs_5_ = f32[768,128]{1,0:T(8,128)S(1)} collective-permute-done((f32[768,128]{1,0:T(8,128)S(1)}, f32[768,128]{1,0:T(8,128)S(1)}, u32[]{:S(2)}, u32[]{:S(2)}) %collective-permute-start.4) | collective-permute-done | bytes 393248 | tf_op jit(solution)/shard_map/ppermute | solution.py:21
  43.8 1.2 %collective-permute-start.5 = (f32[768,128]{1,0:T(8,128)S(1)}, f32[768,128]{1,0:T(8,128)S(1)}, u32[]{:S(2)}, u32[]{:S(2)}) collective-permute-start(f32[768,128]{1,0:T(8,128)S(1)} %collective-permute-done.4.refs_5_), channel_id=1, source_target_pairs={{0,2},{2,0},{1,3},{3,1},{4,6},{6,4},{5,7},{7,5},{8,10},{10,8},{9,1... | collective-permute-start | bytes 1179656 | tf_op jit(solution)/shard_map/ppermute | solution.py:21
  45.1 4.8 %eliminate_u.1.refs_1_ = f32[2,4,128,256]{3,2,1,0:T(8,128)S(1)} custom-call(f32[2,128,384]{2,1,0:T(8,128)S(1)} %get-tuple-element.24.solved_v, f32[2,384,384]{2,1,0:T(8,128)S(1)} %get-tuple-element.25.last), custom_call_target="tpu_custom_call" | custom-call | flops 5000000000 | bytes 1048576 | tf_op jit(solution)/shard_map/eliminate_u/pallas_call | solution.py:333
  49.9 0.0 collective-permute-done.3.refs_2_
  49.9 2.5 %near_columns.1.refs_0_ = f32[2,256,1024]{2,1,0:T(8,128)} custom-call(f32[2,512,512]{2,1,0:T(8,128)S(1)} %bitcast.7, f32[2,4,128,256]{3,2,1,0:T(8,128)S(1)} %eliminate_u.1.refs_1_, f32[1024,128]{1,0:T(8,128)S(1)} %collective-permute-done.3.refs_2_, f32[784,128]{1,0:T(8,128)S(1)} %collective-permute-done.pack.refs_3_, ...), custom_call_target="tpu_custom_call" | custom-call | flops 3000000000 | bytes 1048576 | tf_op jit(solution)/shard_map/near_columns/pallas_call | solution.py:421
  52.4 0.9 %collective-permute-done.5.refs_2_ = f32[768,128]{1,0:T(8,128)S(1)} collective-permute-done((f32[768,128]{1,0:T(8,128)S(1)}, f32[768,128]{1,0:T(8,128)S(1)}, u32[]{:S(2)}, u32[]{:S(2)}) %collective-permute-start.5) | collective-permute-done | bytes 393248 | tf_op jit(solution)/shard_map/ppermute | solution.py:21
  53.2 1.2 %last_columns.1 = f32[2,256,1024]{2,1,0:T(8,128)} custom-call(f32[2,256,1024]{2,1,0:T(8,128)} %near_columns.1.refs_0_, f32[2,4,128,256]{3,2,1,0:T(8,128)S(1)} %eliminate_u.1.refs_1_, f32[768,128]{1,0:T(8,128)S(1)} %collective-permute-done.5.refs_2_), custom_call_target="tpu_custom_call", output_to_operand_aliasing={{}: (0, {})} | custom-call | flops 1500000000 | bytes 1048576 | tf_op jit(solution)/shard_map/last_columns/pallas_call | solution.py:421
Async XLA Ops:
  2.0 22.2 %collective-permute-start = (f32[784,128]{1,0:T(8,128)}, f32[784,128]{1,0:T(8,128)S(1)}, u32[]{:S(2)}, u32[]{:S(2)}) collective-permute-start(f32[784,128]{1,0:T(8,128)} %get-tuple-element.18), channel_id=1, source_target_pairs={{0,8},{8,0},{4,12},{12,4},{1,9},{9,1},{5,13},{13,5},{2,10},{10,2},... | collective-permute-start | bytes 1204232 | tf_op jit(solution)/shard_map/ppermute | solution.py:21
  6.1 9.7 %copy-start = (f32[2,1,1,512,512]{4,3,2,1,0:T(8,128)S(1)}, f32[2,1,1,512,512]{4,3,2,1,0:T(8,128)}, u32[]{:S(2)}) copy-start(f32[2,1,1,512,512]{4,3,2,1,0:T(8,128)} %param.1) | copy-start | bytes 6291460
  6.1 9.7 %copy-start.1 = (f32[528,128]{1,0:T(8,128)S(1)}, f32[528,128]{1,0:T(8,128)}, u32[]{:S(2)}) copy-start(f32[528,128]{1,0:T(8,128)} %get-tuple-element.19.own) | copy-start | bytes 811012
  6.1 8.2 %collective-permute-start.2 = (f32[528,128]{1,0:T(8,128)}, f32[528,128]{1,0:T(8,128)S(1)}, u32[]{:S(2)}, u32[]{:S(2)}) collective-permute-start(f32[528,128]{1,0:T(8,128)} %get-tuple-element.19.own), channel_id=1, source_target_pairs={{0,2},{2,0},{1,3},{3,1},{4,6},{6,4},{5,7},{7,5},{8,10},{10,8},{9,1... | collective-permute-start | bytes 811016 | tf_op jit(solution)/shard_map/ppermute | solution.py:21
  9.9 14.3 %copy-start.2 = (f32[768,128]{1,0:T(8,128)S(1)}, f32[768,128]{1,0:T(8,128)}, u32[]{:S(2)}) copy-start(f32[768,128]{1,0:T(8,128)} %get-tuple-element.29) | copy-start | bytes 1179652
  14.3 35.6 %collective-permute-start.3 = (f32[1024,128]{1,0:T(8,128)}, f32[1024,128]{1,0:T(8,128)S(1)}, u32[]{:S(2)}, u32[]{:S(2)}) collective-permute-start(f32[1024,128]{1,0:T(8,128)} %get-tuple-element.27), channel_id=1, source_target_pairs={{0,2},{2,0},{1,3},{3,1},{4,6},{6,4},{5,7},{7,5},{8,10},{10,8},{9,1... | collective-permute-start | bytes 1572872 | tf_op jit(solution)/shard_map/ppermute | solution.py:21
  24.2 19.6 %collective-permute-start.4 = (f32[768,128]{1,0:T(8,128)S(1)}, f32[768,128]{1,0:T(8,128)S(1)}, u32[]{:S(2)}, u32[]{:S(2)}) collective-permute-start(f32[768,128]{1,0:T(8,128)S(1)} %copy-done.2), channel_id=1, source_target_pairs={{0,8},{8,0},{4,12},{12,4},{1,9},{9,1},{5,13},{13,5},{2,10},{10,2},... | collective-permute-start | bytes 1179656 | tf_op jit(solution)/shard_map/ppermute | solution.py:21
  24.2 11.3 %collective-permute-start.1 = (f32[784,128]{1,0:T(8,128)S(1)}, f32[784,128]{1,0:T(8,128)S(1)}, u32[]{:S(2)}, u32[]{:S(2)}) collective-permute-start(f32[784,128]{1,0:T(8,128)S(1)} %collective-permute-done.pack.refs_3_), channel_id=1, source_target_pairs={{0,2},{2,0},{1,3},{3,1},{4,6},{6,4},{5,7},{7,5},{8,10},{10,8},{9,1... | collective-permute-start | bytes 1204232 | tf_op jit(solution)/shard_map/ppermute | solution.py:21
  43.8 9.4 %collective-permute-start.5 = (f32[768,128]{1,0:T(8,128)S(1)}, f32[768,128]{1,0:T(8,128)S(1)}, u32[]{:S(2)}, u32[]{:S(2)}) collective-permute-start(f32[768,128]{1,0:T(8,128)S(1)} %collective-permute-done.4.refs_5_), channel_id=1, source_target_pairs={{0,2},{2,0},{1,3},{3,1},{4,6},{6,4},{5,7},{7,5},{8,10},{10,8},{9,1... | collective-permute-start | bytes 1179656 | tf_op jit(solution)/shard_map/ppermute | solution.py:21

commit v5 on v4

--- a/solution.py
+++ b/solution.py
@@ -133,29 +133,34 @@
     return 2 * side + SUB
 
 
-def pack_kernel(side, units, tiles, own, sent, own_yy, own_xx, own_yx, sems, unit_sems):
+def pack_kernel(side, units, tiles, own, sent, own_yy, own_xx, sems, unit_sems):
     right, top = role()
     inner, outer = (3 - top, 1 - right), (right, 2 + top)
     waves = own_yy.shape[0]
     tall = height(side)
     copies = []
     for w in range(waves):
-        for n, (i, j, target) in enumerate(((0, 0, own_yy), (1, 1, own_xx), (0, 1, own_yx))):
+        yx = pl.ds(w * tall + side, side)
+        for n, (i, j, target) in enumerate(
+            ((0, 0, own_yy.at[w]), (1, 1, own_xx.at[w]), (0, 1, own.at[yx, :]), (0, 1, sent.at[yx, :]))
+        ):
             source = block_of(tiles, side, w, inner[i], inner[j])
-            copies.append(pltpu.make_async_copy(source, target.at[w], sems.at[3 * w + n]))
+            copies.append(pltpu.make_async_copy(source, target, sems.at[4 * w + n]))
             copies[-1].start()
     others = load_units(tiles, side, inner, outer, units, sent, waves * tall, unit_sems, 0)
     below, diag = square_masks(side)
     for w in range(waves):
-        for copy in copies[3 * w : 3 * w + 3]:
+        for copy in copies[4 * w : 4 * w + 2]:
             copy.wait()
         xx = own_xx[w]
         square = jnp.where(below | diag, own_yy[w], xx)
         line = jnp.broadcast_to(jnp.sum(jnp.where(diag, xx, 0.0), 0, keepdims=True), (SUB, side))
         for target in (own, sent):
             target[w * tall : w * tall + side, :] = square
-            target[w * tall + side : w * tall + 2 * side, :] = own_yx[w]
             target[w * tall + 2 * side : (w + 1) * tall, :] = line
+    for w in range(waves):
+        for copy in copies[4 * w + 2 : 4 * w + 4]:
+            copy.wait()
     for copy in others:
         copy.wait()
 
@@ -180,16 +185,15 @@
         functools.partial(pack_kernel, side, units),
         name="pack",
         out_shape=[
-            jax.ShapeDtypeStruct((rows, side), jnp.float32),
-            jax.ShapeDtypeStruct((rows + len(units) * 2 * side, side), jnp.float32),
+            pltpu.VMEM((rows, side), jnp.float32),
+            pltpu.VMEM((rows + len(units) * 2 * side, side), jnp.float32),
         ],
         in_specs=[pl.BlockSpec(memory_space=pl.ANY)],
         out_specs=[pl.BlockSpec(memory_space=pltpu.VMEM)] * 2,
         scratch_shapes=[
             square,
             square,
-            square,
-            pltpu.SemaphoreType.DMA((3 * waves,)),
+            pltpu.SemaphoreType.DMA((4 * waves,)),
             pltpu.SemaphoreType.DMA((2 * len(units),)),
         ],
         cost_estimate=pl.CostEstimate(flops=work(1.5), bytes_accessed=1 << 20, transcendentals=0),
@@ -441,7 +445,7 @@
     whole, part = couplings(tiles, (units, second))
     cross_0 = swapped(sent, "gx")
     mate_pack = swapped(own, "gy")
-    mate = swapped(after(whole, mate_pack), "gy")
+    mate = swapped(whole, "gy")
 
     def eliminate(kernel, name, shapes, time, **more):
         shapes = [(waves, *shape) for shape in shapes]

time: 54.8 us -> 53.8 us (0.982)
  Pallas kernels: 29.8 us -> 29 us
  starting transfers between devices: 9.87 us -> 9.07 us
  waiting for transfers between devices: 14.6 us -> 15.3 us
    ppermute x6, starting transfers between devices: 9.87 us -> 9.07 us  [swapped(): return lax.ppermute(block, axis, route)]
    pallas_call x1, Pallas kernels: 2 us -> 1.22 us  [packed(): pl.pallas_call(functools.partial(pack_kernel, side, units), name='pack',...]
    ppermute x6, waiting for transfers between devices: 14.6 us -> 15.3 us  [swapped(): return lax.ppermute(block, axis, route)]
  transfers between devices with their start and end apart: 6 -> 6, of which waited for: 5 -> 5; matrix products, arithmetic and copies ran while one was open for 0% -> 0% of each run, Pallas kernels for 49% -> 50%
where the time goes in v5:
time: 53.8 us; the launch traced here: 53.6 us
  Pallas kernels  29 us (54%)
  waiting for transfers between devices  15.3 us (28%)
  starting transfers between devices  9.07 us (17%)
    pallas_call x4, Pallas kernels, call(): pl.pallas_call(kernel, name=name, out_shape=[jax.ShapeDtypeStruct(s, jnp....  21.9 us
    ppermute x6, waiting for transfers between devices, swapped(): return lax.ppermute(block, axis, route)  15.3 us
    ppermute x6, starting transfers between devices, swapped(): return lax.ppermute(block, axis, route)  9.07 us
    pallas_call x2, Pallas kernels, columns_call(): pl.pallas_call(functools.partial(columns_kernel, side, groups, with_own),...  3.63 us
    pallas_call x1, Pallas kernels, couplings(): pl.pallas_call(functools.partial(coupling_kernel, side, groups), name='co...  2.24 us
    pallas_call x1, Pallas kernels, packed(): pl.pallas_call(functools.partial(pack_kernel, side, units), name='pack',...  1.22 us
  transfers between devices with their start and end apart: 6, of which 5 were waited for; matrix products, arithmetic and copies ran while one was open for 0% of the time, Pallas kernels for 50%

profile of v5, /device:TPU:0, one launch (start us, length us, event | category | flops | bytes accessed | tf_op | source)
XLA Modules:
  0.0 53.6 jit_solution(11355273525765258193)
XLA Ops:
  0.0 1.2 %pack.1 = (f32[528,128]{1,0:T(8,128)S(1)}, f32[784,128]{1,0:T(8,128)S(1)}) custom-call(f32[2,512,512]{2,1,0:T(8,128)} %bitcast.4), custom_call_target="tpu_custom_call" | custom-call | flops 1500000000 | bytes 1048576 | tf_op jit(solution)/shard_map/pack/pallas_call | solution.py:184
  1.2 4.1 %collective-permute-start = (f32[784,128]{1,0:T(8,128)S(1)}, f32[784,128]{1,0:T(8,128)S(1)}, u32[]{:S(2)}, u32[]{:S(2)}) collective-permute-start(f32[784,128]{1,0:T(8,128)S(1)} %get-tuple-element.17), channel_id=1, source_target_pairs={{0,8},{8,0},{4,12},{12,4},{1,9},{9,1},{5,13},{13,5},{2,10},{10,2},... | collective-permute-start | bytes 1204232 | tf_op jit(solution)/shard_map/ppermute | solution.py:21
  5.3 0.0 copy-start
  5.3 1.5 %collective-permute-start.2 = (f32[528,128]{1,0:T(8,128)S(1)}, f32[528,128]{1,0:T(8,128)S(1)}, u32[]{:S(2)}, u32[]{:S(2)}) collective-permute-start(f32[528,128]{1,0:T(8,128)S(1)} %get-tuple-element.18.own), channel_id=1, source_target_pairs={{0,2},{2,0},{1,3},{3,1},{4,6},{6,4},{5,7},{7,5},{8,10},{10,8},{9,1... | collective-permute-start | bytes 811016 | tf_op jit(solution)/shard_map/ppermute | solution.py:21
  6.8 2.2 %couplings.1 = (f32[1024,128]{1,0:T(8,128)}, f32[768,128]{1,0:T(8,128)}) custom-call(f32[2,512,512]{2,1,0:T(8,128)} %bitcast.5), custom_call_target="tpu_custom_call" | custom-call | flops 2000000000 | bytes 2097152 | tf_op jit(solution)/shard_map/couplings/pallas_call | solution.py:217
  9.1 0.0 copy-start.1
  9.1 0.7 %collective-permute-start.3 = (f32[1024,128]{1,0:T(8,128)}, f32[1024,128]{1,0:T(8,128)S(1)}, u32[]{:S(2)}, u32[]{:S(2)}) collective-permute-start(f32[1024,128]{1,0:T(8,128)} %get-tuple-element.25), channel_id=1, source_target_pairs={{0,2},{2,0},{1,3},{3,1},{4,6},{6,4},{5,7},{7,5},{8,10},{10,8},{9,1... | collective-permute-start | bytes 1572872 | tf_op jit(solution)/shard_map/ppermute | solution.py:21
  9.8 5.0 %collective-permute-done.2.mate = f32[528,128]{1,0:T(8,128)S(1)} collective-permute-done((f32[528,128]{1,0:T(8,128)S(1)}, f32[528,128]{1,0:T(8,128)S(1)}, u32[]{:S(2)}, u32[]{:S(2)}) %collective-permute-start.2) | collective-permute-done | bytes 270368 | tf_op jit(solution)/shard_map/ppermute | solution.py:21
  14.7 0.0 copy-done
  14.7 6.1 %eliminate_y.1 = (f32[2,128,512]{2,1,0:T(8,128)S(1)}, f32[2,256,512]{2,1,0:T(8,128)S(1)}) custom-call(f32[528,128]{1,0:T(8,128)S(1)} %get-tuple-element.18.own, f32[528,128]{1,0:T(8,128)S(1)} %collective-permute-done.2.mate, f32[2,512,512]{2,1,0:T(8,128)S(1)} %bitcast.6), custom_call_target="tpu_custom_call" | custom-call | flops 1000000000 | bytes 1048576 | tf_op jit(solution)/shard_map/eliminate_y/pallas_call | solution.py:337
  20.8 2.4 %collective-permute-done.pack.refs_3_ = f32[784,128]{1,0:T(8,128)S(1)} collective-permute-done((f32[784,128]{1,0:T(8,128)S(1)}, f32[784,128]{1,0:T(8,128)S(1)}, u32[]{:S(2)}, u32[]{:S(2)}) %collective-permute-start) | collective-permute-done | bytes 401440 | tf_op jit(solution)/shard_map/ppermute | solution.py:21
  23.2 0.0 copy-done.1
  23.2 0.0 collective-permute-start.4
  23.2 1.5 %collective-permute-start.1 = (f32[784,128]{1,0:T(8,128)S(1)}, f32[784,128]{1,0:T(8,128)S(1)}, u32[]{:S(2)}, u32[]{:S(2)}) collective-permute-start(f32[784,128]{1,0:T(8,128)S(1)} %collective-permute-done.pack.refs_3_), channel_id=1, source_target_pairs={{0,2},{2,0},{1,3},{3,1},{4,6},{6,4},{5,7},{7,5},{8,10},{10,8},{9,1... | collective-permute-start | bytes 1204232 | tf_op jit(solution)/shard_map/ppermute | solution.py:21
  24.8 5.7 %eliminate_x.1 = (f32[2,128,512]{2,1,0:T(8,128)S(1)}, f32[2,384,512]{2,1,0:T(8,128)S(1)}) custom-call(f32[784,128]{1,0:T(8,128)S(1)} %collective-permute-done.pack.refs_3_, f32[2,128,512]{2,1,0:T(8,128)S(1)} %get-tuple-element.19.solved_y, f32[2,256,512]{2,1,0:T(8,128)S(1)} %get-tuple-element.20.rest), custom_call_target="tpu_custom_call" | custom-call | flops 6000000000 | bytes 1048576 | tf_op jit(solution)/shard_map/eliminate_x/pallas_call | solution.py:337
  30.5 3.2 %collective-permute-done.1.pack.refs_4_ = f32[784,128]{1,0:T(8,128)S(1)} collective-permute-done((f32[784,128]{1,0:T(8,128)S(1)}, f32[784,128]{1,0:T(8,128)S(1)}, u32[]{:S(2)}, u32[]{:S(2)}) %collective-permute-start.1) | collective-permute-done | bytes 401440 | tf_op jit(solution)/shard_map/ppermute | solution.py:21
  33.7 5.3 %eliminate_v.1 = (f32[2,128,384]{2,1,0:T(8,128)S(1)}, f32[2,384,384]{2,1,0:T(8,128)S(1)}) custom-call(f32[784,128]{1,0:T(8,128)S(1)} %collective-permute-done.1.pack.refs_4_, f32[2,128,512]{2,1,0:T(8,128)S(1)} %get-tuple-element.21.solved_x, f32[2,384,512]{2,1,0:T(8,128)S(1)} %get-tuple-element.22.left), custom_call_target="tpu_custom_call" | custom-call | flops 6000000000 | bytes 1048576 | tf_op jit(solution)/shard_map/eliminate_v/pallas_call | solution.py:337
  39.0 3.8 %collective-permute-done.4.refs_5_ = f32[768,128]{1,0:T(8,128)S(1)} collective-permute-done((f32[768,128]{1,0:T(8,128)S(1)}, f32[768,128]{1,0:T(8,128)S(1)}, u32[]{:S(2)}, u32[]{:S(2)}) %collective-permute-start.4) | collective-permute-done | bytes 393248 | tf_op jit(solution)/shard_map/ppermute | solution.py:21
  42.9 1.2 %collective-permute-start.5 = (f32[768,128]{1,0:T(8,128)S(1)}, f32[768,128]{1,0:T(8,128)S(1)}, u32[]{:S(2)}, u32[]{:S(2)}) collective-permute-start(f32[768,128]{1,0:T(8,128)S(1)} %collective-permute-done.4.refs_5_), channel_id=1, source_target_pairs={{0,2},{2,0},{1,3},{3,1},{4,6},{6,4},{5,7},{7,5},{8,10},{10,8},{9,1... | collective-permute-start | bytes 1179656 | tf_op jit(solution)/shard_map/ppermute | solution.py:21
  44.1 4.8 %eliminate_u.1.refs_1_ = f32[2,4,128,256]{3,2,1,0:T(8,128)S(1)} custom-call(f32[2,128,384]{2,1,0:T(8,128)S(1)} %get-tuple-element.23.solved_v, f32[2,384,384]{2,1,0:T(8,128)S(1)} %get-tuple-element.24.last), custom_call_target="tpu_custom_call" | custom-call | flops 5000000000 | bytes 1048576 | tf_op jit(solution)/shard_map/eliminate_u/pallas_call | solution.py:337
  48.9 0.0 collective-permute-done.3.refs_2_
  48.9 2.5 %near_columns.1.refs_0_ = f32[2,256,1024]{2,1,0:T(8,128)} custom-call(f32[2,512,512]{2,1,0:T(8,128)S(1)} %bitcast.7, f32[2,4,128,256]{3,2,1,0:T(8,128)S(1)} %eliminate_u.1.refs_1_, f32[1024,128]{1,0:T(8,128)S(1)} %collective-permute-done.3.refs_2_, f32[784,128]{1,0:T(8,128)S(1)} %collective-permute-done.pack.refs_3_, ...), custom_call_target="tpu_custom_call" | custom-call | flops 3000000000 | bytes 1048576 | tf_op jit(solution)/shard_map/near_columns/pallas_call | solution.py:425
  51.4 0.9 %collective-permute-done.5.refs_2_ = f32[768,128]{1,0:T(8,128)S(1)} collective-permute-done((f32[768,128]{1,0:T(8,128)S(1)}, f32[768,128]{1,0:T(8,128)S(1)}, u32[]{:S(2)}, u32[]{:S(2)}) %collective-permute-start.5) | collective-permute-done | bytes 393248 | tf_op jit(solution)/shard_map/ppermute | solution.py:21
  52.2 1.2 %last_columns.1 = f32[2,256,1024]{2,1,0:T(8,128)} custom-call(f32[2,256,1024]{2,1,0:T(8,128)} %near_columns.1.refs_0_, f32[2,4,128,256]{3,2,1,0:T(8,128)S(1)} %eliminate_u.1.refs_1_, f32[768,128]{1,0:T(8,128)S(1)} %collective-permute-done.5.refs_2_), custom_call_target="tpu_custom_call", output_to_operand_aliasing={{}: (0, {})} | custom-call | flops 1500000000 | bytes 1048576 | tf_op jit(solution)/shard_map/last_columns/pallas_call | solution.py:425
Async XLA Ops:
  1.2 22.0 %collective-permute-start = (f32[784,128]{1,0:T(8,128)S(1)}, f32[784,128]{1,0:T(8,128)S(1)}, u32[]{:S(2)}, u32[]{:S(2)}) collective-permute-start(f32[784,128]{1,0:T(8,128)S(1)} %get-tuple-element.17), channel_id=1, source_target_pairs={{0,8},{8,0},{4,12},{12,4},{1,9},{9,1},{5,13},{13,5},{2,10},{10,2},... | collective-permute-start | bytes 1204232 | tf_op jit(solution)/shard_map/ppermute | solution.py:21
  5.3 9.4 %copy-start = (f32[2,1,1,512,512]{4,3,2,1,0:T(8,128)S(1)}, f32[2,1,1,512,512]{4,3,2,1,0:T(8,128)}, u32[]{:S(2)}) copy-start(f32[2,1,1,512,512]{4,3,2,1,0:T(8,128)} %param.1) | copy-start | bytes 6291460
  5.3 9.4 %collective-permute-start.2 = (f32[528,128]{1,0:T(8,128)S(1)}, f32[528,128]{1,0:T(8,128)S(1)}, u32[]{:S(2)}, u32[]{:S(2)}) collective-permute-start(f32[528,128]{1,0:T(8,128)S(1)} %get-tuple-element.18.own), channel_id=1, source_target_pairs={{0,2},{2,0},{1,3},{3,1},{4,6},{6,4},{5,7},{7,5},{8,10},{10,8},{9,1... | collective-permute-start | bytes 811016 | tf_op jit(solution)/shard_map/ppermute | solution.py:21
  9.1 14.2 %copy-start.1 = (f32[768,128]{1,0:T(8,128)S(1)}, f32[768,128]{1,0:T(8,128)}, u32[]{:S(2)}) copy-start(f32[768,128]{1,0:T(8,128)} %get-tuple-element.27) | copy-start | bytes 1179652
  9.1 39.8 %collective-permute-start.3 = (f32[1024,128]{1,0:T(8,128)}, f32[1024,128]{1,0:T(8,128)S(1)}, u32[]{:S(2)}, u32[]{:S(2)}) collective-permute-start(f32[1024,128]{1,0:T(8,128)} %get-tuple-element.25), channel_id=1, source_target_pairs={{0,2},{2,0},{1,3},{3,1},{4,6},{6,4},{5,7},{7,5},{8,10},{10,8},{9,1... | collective-permute-start | bytes 1572872 | tf_op jit(solution)/shard_map/ppermute | solution.py:21
  23.2 19.6 %collective-permute-start.4 = (f32[768,128]{1,0:T(8,128)S(1)}, f32[768,128]{1,0:T(8,128)S(1)}, u32[]{:S(2)}, u32[]{:S(2)}) collective-permute-start(f32[768,128]{1,0:T(8,128)S(1)} %copy-done.1), channel_id=1, source_target_pairs={{0,8},{8,0},{4,12},{12,4},{1,9},{9,1},{5,13},{13,5},{2,10},{10,2},... | collective-permute-start | bytes 1179656 | tf_op jit(solution)/shard_map/ppermute | solution.py:21
  23.2 10.5 %collective-permute-start.1 = (f32[784,128]{1,0:T(8,128)S(1)}, f32[784,128]{1,0:T(8,128)S(1)}, u32[]{:S(2)}, u32[]{:S(2)}) collective-permute-start(f32[784,128]{1,0:T(8,128)S(1)} %collective-permute-done.pack.refs_3_), channel_id=1, source_target_pairs={{0,2},{2,0},{1,3},{3,1},{4,6},{6,4},{5,7},{7,5},{8,10},{10,8},{9,1... | collective-permute-start | bytes 1204232 | tf_op jit(solution)/shard_map/ppermute | solution.py:21
  42.9 9.4 %collective-permute-start.5 = (f32[768,128]{1,0:T(8,128)S(1)}, f32[768,128]{1,0:T(8,128)S(1)}, u32[]{:S(2)}, u32[]{:S(2)}) collective-permute-start(f32[768,128]{1,0:T(8,128)S(1)} %collective-permute-done.4.refs_5_), channel_id=1, source_target_pairs={{0,2},{2,0},{1,3},{3,1},{4,6},{6,4},{5,7},{7,5},{8,10},{10,8},{9,1... | collective-permute-start | bytes 1179656 | tf_op jit(solution)/shard_map/ppermute | solution.py:21

commit v6 on v5

--- a/solution.py
+++ b/solution.py
@@ -439,10 +439,10 @@
     tiles = children[:, 0, 0]
     waves, side = tiles.shape[0], tiles.shape[1] // 4
     units = tuple(range(2 * waves))
-    first, second = units[:1], units[1:]
+    first, second, third = units[:1], units[1:3], units[3:]
     base = waves * height(side)
     own, sent = packed(tiles, first)
-    whole, part = couplings(tiles, (units, second))
+    whole, part_1, part_2 = couplings(tiles, (units, second, third))
     cross_0 = swapped(sent, "gx")
     mate_pack = swapped(own, "gy")
     mate = swapped(whole, "gy")
@@ -456,7 +456,8 @@
     solved_y, rest = eliminate(
         first_kernel, "eliminate_y", [(side, full), (2 * side, full)], 1, tiles=tiles, scratch=loads
     )(own, mate_pack)
-    cross_1 = swapped(after(part, (cross_0, solved_y)), "gx")
+    cross_1 = swapped(after(part_1, (cross_0, solved_y)), "gx")
+    cross_2 = swapped(after(part_2, (cross_0, solved_y)), "gx")
     far_0 = swapped(cross_0, "gy")
     solved_x, left = eliminate(second_kernel, "eliminate_x", [(side, full), (3 * side, full)], 6)(
         cross_0, solved_y, rest
@@ -464,6 +465,7 @@
     solved_v, last = eliminate(third_kernel, "eliminate_v", [(side, 3 * side), (3 * side, 3 * side)], 6)(
         far_0, solved_x, left
     )
+    far_2 = swapped(after(cross_2, solved_v), "gy")
     far_1 = swapped(after(cross_1, solved_v), "gy")
     (held,) = eliminate(fourth_kernel, "eliminate_u", [(4, side, 2 * side)], 5)(solved_v, last)
     near = columns_call(
@@ -471,10 +473,10 @@
         3,
         tiles,
         held,
-        [(MATE, units, mate, 0), (CROSS, first, cross_0, base), (FAR, first, far_0, base), (CROSS, second, cross_1, 0)],
+        [(MATE, units, mate, 0), (CROSS, first, cross_0, base), (FAR, first, far_0, base), (CROSS, second, cross_1, 0), (CROSS, third, cross_2, 0)],
         True,
     )
-    merged = columns_call("last_columns", 1.5, near, held, [(FAR, second, far_1, 0)], False)
+    merged = columns_call("last_columns", 1.5, near, held, [(FAR, third, far_2, 0), (FAR, second, far_1, 0)], False)
     return merged[:, None, None]
 
 

time: 53.8 us -> 53.9 us (level)
  waiting for transfers between devices: 15.3 us -> 11.5 us
  starting transfers between devices: 9.07 us -> 12.8 us
    ppermute x6 -> x8, waiting for transfers between devices: 15.3 us -> 11.5 us  [swapped(): return lax.ppermute(block, axis, route)]
    ppermute x6 -> x8, starting transfers between devices: 9.07 us -> 12.8 us  [swapped(): return lax.ppermute(block, axis, route)]
  transfers between devices with their start and end apart: 6 -> 8, of which waited for: 5 -> 4; matrix products, arithmetic and copies ran while one was open for 0% -> 0% of each run, Pallas kernels for 50% -> 50%
where the time goes in v6:
time: 53.9 us; the launch traced here: 53.7 us
  Pallas kernels  29.1 us (54%)
  starting transfers between devices  12.8 us (24%)
  waiting for transfers between devices  11.5 us (21%)
    pallas_call x4, Pallas kernels, call(): pl.pallas_call(kernel, name=name, out_shape=[jax.ShapeDtypeStruct(s, jnp....  21.9 us
    ppermute x8, starting transfers between devices, swapped(): return lax.ppermute(block, axis, route)  12.8 us
    ppermute x8, waiting for transfers between devices, swapped(): return lax.ppermute(block, axis, route)  11.5 us
    pallas_call x2, Pallas kernels, columns_call(): pl.pallas_call(functools.partial(columns_kernel, side, groups, with_own),...  3.78 us
    pallas_call x1, Pallas kernels, couplings(): pl.pallas_call(functools.partial(coupling_kernel, side, groups), name='co...  2.24 us
    pallas_call x1, Pallas kernels, packed(): pl.pallas_call(functools.partial(pack_kernel, side, units), name='pack',...  1.22 us
  transfers between devices with their start and end apart: 8, of which 4 were waited for; matrix products, arithmetic and copies ran while one was open for 0% of the time, Pallas kernels for 50%

profile of v6, /device:TPU:0, one launch (start us, length us, event | category | flops | bytes accessed | tf_op | source)
XLA Modules:
  0.0 53.7 jit_solution(11751835779184657074)
XLA Ops:
  0.0 1.2 %pack.1 = (f32[528,128]{1,0:T(8,128)S(1)}, f32[784,128]{1,0:T(8,128)S(1)}) custom-call(f32[2,512,512]{2,1,0:T(8,128)} %bitcast.4), custom_call_target="tpu_custom_call" | custom-call | flops 1500000000 | bytes 1048576 | tf_op jit(solution)/shard_map/pack/pallas_call | solution.py:184
  1.2 4.1 %collective-permute-start = (f32[784,128]{1,0:T(8,128)S(1)}, f32[784,128]{1,0:T(8,128)S(1)}, u32[]{:S(2)}, u32[]{:S(2)}) collective-permute-start(f32[784,128]{1,0:T(8,128)S(1)} %get-tuple-element.20), channel_id=1, source_target_pairs={{0,8},{8,0},{4,12},{12,4},{1,9},{9,1},{5,13},{13,5},{2,10},{10,2},... | collective-permute-start | bytes 1204232 | tf_op jit(solution)/shard_map/ppermute | solution.py:21
  5.3 0.0 copy-start
  5.3 1.5 %collective-permute-start.2 = (f32[528,128]{1,0:T(8,128)S(1)}, f32[528,128]{1,0:T(8,128)S(1)}, u32[]{:S(2)}, u32[]{:S(2)}) collective-permute-start(f32[528,128]{1,0:T(8,128)S(1)} %get-tuple-element.21.own), channel_id=1, source_target_pairs={{0,2},{2,0},{1,3},{3,1},{4,6},{6,4},{5,7},{7,5},{8,10},{10,8},{9,1... | collective-permute-start | bytes 811016 | tf_op jit(solution)/shard_map/ppermute | solution.py:21
  6.8 2.2 %couplings.1 = (f32[1024,128]{1,0:T(8,128)}, f32[512,128]{1,0:T(8,128)}, f32[256,128]{1,0:T(8,128)}) custom-call(f32[2,512,512]{2,1,0:T(8,128)} %bitcast.5), custom_call_target="tpu_custom_call" | custom-call | flops 2000000000 | bytes 2097152 | tf_op jit(solution)/shard_map/couplings/pallas_call | solution.py:217
  9.1 0.0 copy-start.2
  9.1 0.0 copy-start.1
  9.1 0.7 %collective-permute-start.3 = (f32[1024,128]{1,0:T(8,128)}, f32[1024,128]{1,0:T(8,128)S(1)}, u32[]{:S(2)}, u32[]{:S(2)}) collective-permute-start(f32[1024,128]{1,0:T(8,128)} %get-tuple-element.28), channel_id=1, source_target_pairs={{0,2},{2,0},{1,3},{3,1},{4,6},{6,4},{5,7},{7,5},{8,10},{10,8},{9,1... | collective-permute-start | bytes 1572872 | tf_op jit(solution)/shard_map/ppermute | solution.py:21
  9.8 5.0 %collective-permute-done.2.mate = f32[528,128]{1,0:T(8,128)S(1)} collective-permute-done((f32[528,128]{1,0:T(8,128)S(1)}, f32[528,128]{1,0:T(8,128)S(1)}, u32[]{:S(2)}, u32[]{:S(2)}) %collective-permute-start.2) | collective-permute-done | bytes 270368 | tf_op jit(solution)/shard_map/ppermute | solution.py:21
  14.7 0.0 copy-done
  14.7 6.1 %eliminate_y.1 = (f32[2,128,512]{2,1,0:T(8,128)S(1)}, f32[2,256,512]{2,1,0:T(8,128)S(1)}) custom-call(f32[528,128]{1,0:T(8,128)S(1)} %get-tuple-element.21.own, f32[528,128]{1,0:T(8,128)S(1)} %collective-permute-done.2.mate, f32[2,512,512]{2,1,0:T(8,128)S(1)} %bitcast.6), custom_call_target="tpu_custom_call" | custom-call | flops 1000000000 | bytes 1048576 | tf_op jit(solution)/shard_map/eliminate_y/pallas_call | solution.py:337
  20.8 2.4 %collective-permute-done.pack.refs_3_ = f32[784,128]{1,0:T(8,128)S(1)} collective-permute-done((f32[784,128]{1,0:T(8,128)S(1)}, f32[784,128]{1,0:T(8,128)S(1)}, u32[]{:S(2)}, u32[]{:S(2)}) %collective-permute-start) | collective-permute-done | bytes 401440 | tf_op jit(solution)/shard_map/ppermute | solution.py:21
  23.2 0.0 copy-done.2
  23.2 0.0 collective-permute-start.5
  23.2 0.0 copy-done.1
  23.2 2.9 %collective-permute-start.4 = (f32[512,128]{1,0:T(8,128)S(1)}, f32[512,128]{1,0:T(8,128)S(1)}, u32[]{:S(2)}, u32[]{:S(2)}) collective-permute-start(f32[512,128]{1,0:T(8,128)S(1)} %copy-done.1), channel_id=1, source_target_pairs={{0,8},{8,0},{4,12},{12,4},{1,9},{9,1},{5,13},{13,5},{2,10},{10,2},... | collective-permute-start | bytes 786440 | tf_op jit(solution)/shard_map/ppermute | solution.py:21
  26.2 1.5 %collective-permute-start.1 = (f32[784,128]{1,0:T(8,128)S(1)}, f32[784,128]{1,0:T(8,128)S(1)}, u32[]{:S(2)}, u32[]{:S(2)}) collective-permute-start(f32[784,128]{1,0:T(8,128)S(1)} %collective-permute-done.pack.refs_3_), channel_id=1, source_target_pairs={{0,2},{2,0},{1,3},{3,1},{4,6},{6,4},{5,7},{7,5},{8,10},{10,8},{9,1... | collective-permute-start | bytes 1204232 | tf_op jit(solution)/shard_map/ppermute | solution.py:21
  27.7 5.7 %eliminate_x.1 = (f32[2,128,512]{2,1,0:T(8,128)S(1)}, f32[2,384,512]{2,1,0:T(8,128)S(1)}) custom-call(f32[784,128]{1,0:T(8,128)S(1)} %collective-permute-done.pack.refs_3_, f32[2,128,512]{2,1,0:T(8,128)S(1)} %get-tuple-element.22.solved_y, f32[2,256,512]{2,1,0:T(8,128)S(1)} %get-tuple-element.23.rest), custom_call_target="tpu_custom_call" | custom-call | flops 6000000000 | bytes 1048576 | tf_op jit(solution)/shard_map/eliminate_x/pallas_call | solution.py:337
  33.5 2.6 %collective-permute-done.1.pack.refs_4_ = f32[784,128]{1,0:T(8,128)S(1)} collective-permute-done((f32[784,128]{1,0:T(8,128)S(1)}, f32[784,128]{1,0:T(8,128)S(1)}, u32[]{:S(2)}, u32[]{:S(2)}) %collective-permute-start.1) | collective-permute-done | bytes 401440 | tf_op jit(solution)/shard_map/ppermute | solution.py:21
  36.1 5.3 %eliminate_v.1 = (f32[2,128,384]{2,1,0:T(8,128)S(1)}, f32[2,384,384]{2,1,0:T(8,128)S(1)}) custom-call(f32[784,128]{1,0:T(8,128)S(1)} %collective-permute-done.1.pack.refs_4_, f32[2,128,512]{2,1,0:T(8,128)S(1)} %get-tuple-element.24.solved_x, f32[2,384,512]{2,1,0:T(8,128)S(1)} %get-tuple-element.25.left), custom_call_target="tpu_custom_call" | custom-call | flops 6000000000 | bytes 1048576 | tf_op jit(solution)/shard_map/eliminate_v/pallas_call | solution.py:337
  41.4 1.5 %collective-permute-done.4.refs_5_ = f32[512,128]{1,0:T(8,128)S(1)} collective-permute-done((f32[512,128]{1,0:T(8,128)S(1)}, f32[512,128]{1,0:T(8,128)S(1)}, u32[]{:S(2)}, u32[]{:S(2)}) %collective-permute-start.4) | collective-permute-done | bytes 262176 | tf_op jit(solution)/shard_map/ppermute | solution.py:21
  42.9 0.0 collective-permute-done.5.refs_6_
  42.9 1.2 %collective-permute-start.6 = (f32[256,128]{1,0:T(8,128)S(1)}, f32[256,128]{1,0:T(8,128)S(1)}, u32[]{:S(2)}, u32[]{:S(2)}) collective-permute-start(f32[256,128]{1,0:T(8,128)S(1)} %collective-permute-done.5.refs_6_), channel_id=1, source_target_pairs={{0,2},{2,0},{1,3},{3,1},{4,6},{6,4},{5,7},{7,5},{8,10},{10,8},{9,1... | collective-permute-start | bytes 393224 | tf_op jit(solution)/shard_map/ppermute | solution.py:21
  44.1 0.8 %collective-permute-start.7 = (f32[512,128]{1,0:T(8,128)S(1)}, f32[512,128]{1,0:T(8,128)S(1)}, u32[]{:S(2)}, u32[]{:S(2)}) collective-permute-start(f32[512,128]{1,0:T(8,128)S(1)} %collective-permute-done.4.refs_5_), channel_id=1, source_target_pairs={{0,2},{2,0},{1,3},{3,1},{4,6},{6,4},{5,7},{7,5},{8,10},{10,8},{9,1... | collective-permute-start | bytes 786440 | tf_op jit(solution)/shard_map/ppermute | solution.py:21
  44.9 4.8 %eliminate_u.1.refs_1_ = f32[2,4,128,256]{3,2,1,0:T(8,128)S(1)} custom-call(f32[2,128,384]{2,1,0:T(8,128)S(1)} %get-tuple-element.26.solved_v, f32[2,384,384]{2,1,0:T(8,128)S(1)} %get-tuple-element.27.last), custom_call_target="tpu_custom_call" | custom-call | flops 5000000000 | bytes 1048576 | tf_op jit(solution)/shard_map/eliminate_u/pallas_call | solution.py:337
  49.7 0.0 collective-permute-done.3.refs_2_
  49.7 2.6 %near_columns.1.refs_0_ = f32[2,256,1024]{2,1,0:T(8,128)} custom-call(f32[2,512,512]{2,1,0:T(8,128)S(1)} %bitcast.7, f32[2,4,128,256]{3,2,1,0:T(8,128)S(1)} %eliminate_u.1.refs_1_, f32[1024,128]{1,0:T(8,128)S(1)} %collective-permute-done.3.refs_2_, f32[784,128]{1,0:T(8,128)S(1)} %collective-permute-done.pack.refs_3_, ...), custom_call_target="tpu_custom_call" | custom-call | flops 3000000000 | bytes 1048576 | tf_op jit(solution)/shard_map/near_columns/pallas_call | solution.py:425
  52.2 0.0 collective-permute-done.6.refs_2_
  52.3 0.0 collective-permute-done.7.refs_3_
  52.3 1.2 %last_columns.1 = f32[2,256,1024]{2,1,0:T(8,128)} custom-call(f32[2,256,1024]{2,1,0:T(8,128)} %near_columns.1.refs_0_, f32[2,4,128,256]{3,2,1,0:T(8,128)S(1)} %eliminate_u.1.refs_1_, f32[256,128]{1,0:T(8,128)S(1)} %collective-permute-done.6.refs_2_, f32[512,128]{1,0:T(8,128)S(1)} %collective-permute-done.7.refs_3_), custom_call_target="tpu_custom_call", output_to_operand_aliasing={{}: (0, {})} | custom-call | flops 1500000000 | bytes 1048576 | tf_op jit(solution)/shard_map/last_columns/pallas_call | solution.py:425
Async XLA Ops:
  1.2 22.0 %collective-permute-start = (f32[784,128]{1,0:T(8,128)S(1)}, f32[784,128]{1,0:T(8,128)S(1)}, u32[]{:S(2)}, u32[]{:S(2)}) collective-permute-start(f32[784,128]{1,0:T(8,128)S(1)} %get-tuple-element.20), channel_id=1, source_target_pairs={{0,8},{8,0},{4,12},{12,4},{1,9},{9,1},{5,13},{13,5},{2,10},{10,2},... | collective-permute-start | bytes 1204232 | tf_op jit(solution)/shard_map/ppermute | solution.py:21
  5.3 9.4 %copy-start = (f32[2,1,1,512,512]{4,3,2,1,0:T(8,128)S(1)}, f32[2,1,1,512,512]{4,3,2,1,0:T(8,128)}, u32[]{:S(2)}) copy-start(f32[2,1,1,512,512]{4,3,2,1,0:T(8,128)} %param.1) | copy-start | bytes 6291460
  5.3 9.4 %collective-permute-start.2 = (f32[528,128]{1,0:T(8,128)S(1)}, f32[528,128]{1,0:T(8,128)S(1)}, u32[]{:S(2)}, u32[]{:S(2)}) collective-permute-start(f32[528,128]{1,0:T(8,128)S(1)} %get-tuple-element.21.own), channel_id=1, source_target_pairs={{0,2},{2,0},{1,3},{3,1},{4,6},{6,4},{5,7},{7,5},{8,10},{10,8},{9,1... | collective-permute-start | bytes 811016 | tf_op jit(solution)/shard_map/ppermute | solution.py:21
  9.1 14.2 %copy-start.2 = (f32[256,128]{1,0:T(8,128)S(1)}, f32[256,128]{1,0:T(8,128)}, u32[]{:S(2)}) copy-start(f32[256,128]{1,0:T(8,128)} %get-tuple-element.32) | copy-start | bytes 393220
  9.1 14.2 %copy-start.1 = (f32[512,128]{1,0:T(8,128)S(1)}, f32[512,128]{1,0:T(8,128)}, u32[]{:S(2)}) copy-start(f32[512,128]{1,0:T(8,128)} %get-tuple-element.30) | copy-start | bytes 786436
  9.1 40.6 %collective-permute-start.3 = (f32[1024,128]{1,0:T(8,128)}, f32[1024,128]{1,0:T(8,128)S(1)}, u32[]{:S(2)}, u32[]{:S(2)}) collective-permute-start(f32[1024,128]{1,0:T(8,128)} %get-tuple-element.28), channel_id=1, source_target_pairs={{0,2},{2,0},{1,3},{3,1},{4,6},{6,4},{5,7},{7,5},{8,10},{10,8},{9,1... | collective-permute-start | bytes 1572872 | tf_op jit(solution)/shard_map/ppermute | solution.py:21
  23.2 19.6 %collective-permute-start.5 = (f32[256,128]{1,0:T(8,128)S(1)}, f32[256,128]{1,0:T(8,128)S(1)}, u32[]{:S(2)}, u32[]{:S(2)}) collective-permute-start(f32[256,128]{1,0:T(8,128)S(1)} %copy-done.2), channel_id=1, source_target_pairs={{0,8},{8,0},{4,12},{12,4},{1,9},{9,1},{5,13},{13,5},{2,10},{10,2},... | collective-permute-start | bytes 393224 | tf_op jit(solution)/shard_map/ppermute | solution.py:21
  23.2 19.6 %collective-permute-start.4 = (f32[512,128]{1,0:T(8,128)S(1)}, f32[512,128]{1,0:T(8,128)S(1)}, u32[]{:S(2)}, u32[]{:S(2)}) collective-permute-start(f32[512,128]{1,0:T(8,128)S(1)} %copy-done.1), channel_id=1, source_target_pairs={{0,8},{8,0},{4,12},{12,4},{1,9},{9,1},{5,13},{13,5},{2,10},{10,2},... | collective-permute-start | bytes 786440 | tf_op jit(solution)/shard_map/ppermute | solution.py:21
  26.2 9.9 %collective-permute-start.1 = (f32[784,128]{1,0:T(8,128)S(1)}, f32[784,128]{1,0:T(8,128)S(1)}, u32[]{:S(2)}, u32[]{:S(2)}) collective-permute-start(f32[784,128]{1,0:T(8,128)S(1)} %collective-permute-done.pack.refs_3_), channel_id=1, source_target_pairs={{0,2},{2,0},{1,3},{3,1},{4,6},{6,4},{5,7},{7,5},{8,10},{10,8},{9,1... | collective-permute-start | bytes 1204232 | tf_op jit(solution)/shard_map/ppermute | solution.py:21
  42.9 9.4 %collective-permute-start.6 = (f32[256,128]{1,0:T(8,128)S(1)}, f32[256,128]{1,0:T(8,128)S(1)}, u32[]{:S(2)}, u32[]{:S(2)}) collective-permute-start(f32[256,128]{1,0:T(8,128)S(1)} %collective-permute-done.5.refs_6_), channel_id=1, source_target_pairs={{0,2},{2,0},{1,3},{3,1},{4,6},{6,4},{5,7},{7,5},{8,10},{10,8},{9,1... | collective-permute-start | bytes 393224 | tf_op jit(solution)/shard_map/ppermute | solution.py:21
  44.1 8.2 %collective-permute-start.7 = (f32[512,128]{1,0:T(8,128)S(1)}, f32[512,128]{1,0:T(8,128)S(1)}, u32[]{:S(2)}, u32[]{:S(2)}) collective-permute-start(f32[512,128]{1,0:T(8,128)S(1)} %collective-permute-done.4.refs_5_), channel_id=1, source_target_pairs={{0,2},{2,0},{1,3},{3,1},{4,6},{6,4},{5,7},{7,5},{8,10},{10,8},{9,1... | collective-permute-start | bytes 786440 | tf_op jit(solution)/shard_map/ppermute | solution.py:21
